TPU v7x, 32 devices: a whole 2x2x4 slice. The times are simulated.
32 devices in a mesh: sector: 4 (over y, x), shard: 8 (over z, core).
Axes of the slice: x: 2, y: 2, z: 4, core: 2. Of those that a mesh axis runs over, the one named last changes fastest.
Arguments:
- wavefunction: bfloat16 [4, 768, 12288], P('sector', None, 'shard'), may hold values from -6 to 6
- left_environment: bfloat16 [2, 4, 768, 768], P(None, 'sector', 'shard'), may hold values from -0.21875 to 0.21875
- right_environment: bfloat16 [2, 4, 768, 768], P(None, 'sector', 'shard'), may hold values from -0.21875 to 0.21875
- targets: int32 [2, 4], replicated, may hold values from 0 to 3
- bond_sizes: int32 [2, 4], replicated, may hold values from 384 to 768, as said below
Outputs:
- applied: bfloat16 [4, 768, 12288], P('sector', 'shard')
Inputs may be any that keep to these rules, and one draw needn't show every extreme that they name: `bond_sizes`: each of the two rows reaches 768 at some block.
All inputs are finite; a program needn't handle non-finite values.
Results may differ from a plain program's by a relative error of at most 0.0055.
Values may be sent and summed in bfloat16 or wider, within the bound.
No kernel may reach another device: no remote copies, remote signals or barrier semaphores. Data moves between devices by JAX's collectives and lax.ppermute only.
A program may use at most 64 MiB of HBM per device.

v0:
```python
import functools
import math

import jax
import jax.numpy as jnp
from jax import lax
from jax.experimental import pallas as pl
from jax.experimental.pallas import tpu as pltpu
from jax.sharding import PartitionSpec as P


def is_pow2(n):
    return n & (n - 1) == 0


def exchange(x, axis, offset):
    size = lax.axis_size(axis)
    return lax.ppermute(x, axis, [(a, a ^ offset) for a in range(size)])


def gather_pieces(piece):
    pieces = []
    for m in range(0, lax.axis_size("shard"), 2):
        near = exchange(piece, "shard", m) if m else piece
        pieces += [near, exchange(near, "shard", 1)]
    return pieces


def live_mask(shape, rows_live, cols_live, row_start):
    row = lax.broadcasted_iota(jnp.int32, shape, 0) + row_start
    col = lax.broadcasted_iota(jnp.int32, shape, 1)
    return (row < rows_live) & (col < cols_live)


def mask_left_kernel(targets, sizes, e_ref, *outs):
    sector, shard = lax.axis_index("sector"), lax.axis_index("shard")
    rows, bond = outs[0].shape
    for c, out in enumerate(outs):
        keep = live_mask((rows, bond), sizes[0, targets[c, sector]], sizes[0, sector], shard * rows)
        out[...] = jnp.where(keep, e_ref[c], 0).astype(out.dtype)


def mask_right_kernel(targets, sizes, *refs, blocks, channel):
    sources, out = refs[:blocks], refs[blocks]
    sector, shard = lax.axis_index("sector"), lax.axis_index("shard")
    target = targets[channel, sector]
    live = sizes[1, target]
    keep = live_mask(out.shape, live, jnp.minimum(live, sizes[1, sector]), shard * out.shape[0])
    for k in range(blocks):
        @pl.when(target == sector ^ k)
        def _(k=k):
            out[...] = jnp.where(keep, sources[k][...], 0).astype(out.dtype)


def masked(kernel, outs, targets, sizes, *arrays):
    rows, bond = arrays[0].shape[-2:]
    full, scalars = pl.BlockSpec(memory_space=pltpu.VMEM), pl.BlockSpec(memory_space=pltpu.SMEM)
    return pl.pallas_call(
        kernel,
        out_shape=[jax.ShapeDtypeStruct((rows, bond), jnp.bfloat16)] * outs,
        in_specs=[scalars] * 2 + [full] * len(arrays),
        out_specs=[full] * outs,
    )(targets, sizes, *arrays)


def products_kernel(*refs, shards_n, row_parts, col_parts, phys):
    e_refs, f_refs = refs[:shards_n], refs[shards_n:2 * shards_n]
    psi_ref = refs[2 * shards_n]
    y_refs = refs[2 * shards_n + 1:-2]
    left_ref, right_ref = refs[-2:]
    rows, bond = e_refs[0].shape
    sub = rows // row_parts
    block = shards_n * sub
    sector, shard = lax.axis_index("sector"), lax.axis_index("shard")
    own_row, own_col = sector // col_parts, sector % col_parts
    for m in range(shards_n):
        right_ref[pl.ds(pl.multiple_of((shard ^ m) * rows, 16), rows), :] = f_refs[m][...]
        for h in range(row_parts):
            at = pl.multiple_of((own_row ^ h) * sub, 16)
            left_ref[h * block + m * sub:h * block + (m + 1) * sub, :] = e_refs[m][pl.ds(at, sub), :]
    for g in range(col_parts):
        for p in range(phys):
            at = pl.multiple_of(((own_col ^ g) * phys + p) * bond, 128)
            half = jnp.dot(left_ref[...], psi_ref[:, pl.ds(at, bond)], preferred_element_type=jnp.float32)
            y = lax.dot_general(half.astype(jnp.bfloat16), right_ref[...], (((1,), (1,)), ((), ())),
                                preferred_element_type=jnp.float32).astype(jnp.bfloat16)
            for h in range(row_parts):
                y_refs[h * col_parts + g][:, p * bond:(p + 1) * bond] = y[h * block:(h + 1) * block]


def products(e_pieces, f_pieces, psi, row_parts, col_parts):
    shards_n = len(e_pieces)
    rows, bond = e_pieces[0].shape
    phys = psi.shape[1] // bond // col_parts
    out = jax.ShapeDtypeStruct((shards_n * rows // row_parts, phys * bond), jnp.bfloat16)
    full = pl.BlockSpec(memory_space=pltpu.VMEM)
    return pl.pallas_call(
        functools.partial(products_kernel, shards_n=shards_n, row_parts=row_parts, col_parts=col_parts,
                          phys=phys),
        out_shape=[out] * (row_parts * col_parts),
        in_specs=[full] * (2 * shards_n + 1),
        out_specs=[full] * (row_parts * col_parts),
        scratch_shapes=[pltpu.VMEM((bond, bond), jnp.bfloat16)] * 2,
        name="products",
    )(*e_pieces, *f_pieces, psi)


def sum_kernel(targets, *refs, blocks):
    sources, outs, acc = refs[:-blocks - 1], refs[-blocks - 1:-1], refs[-1]
    sector = lax.axis_index("sector")
    acc[...] = jnp.zeros_like(acc)
    for n, ref in enumerate(sources):
        j = targets[n // blocks, sector ^ (n % blocks)] ^ sector
        acc[j] = acc[j] + ref[...].astype(jnp.float32)
    for j in range(blocks):
        outs[j][...] = acc[j].astype(jnp.bfloat16)


def destination_sums(targets, sources, blocks, steps):
    rows, width = sources[0].shape
    spec = pl.BlockSpec((rows // steps, width), lambda n: (n, 0))
    return pl.pallas_call(
        functools.partial(sum_kernel, blocks=blocks),
        grid=(steps,),
        out_shape=[jax.ShapeDtypeStruct((rows, width), jnp.bfloat16)] * blocks,
        in_specs=[pl.BlockSpec(memory_space=pltpu.SMEM)] + [spec] * len(sources),
        out_specs=[spec] * blocks,
        scratch_shapes=[pltpu.VMEM((blocks, rows // steps, width), jnp.float32)],
        name="destination_sums",
    )(targets, *sources)


def fast(*arrays):
    return apply_blocks(*arrays)


def apply_blocks(wavefunction, left_environment, right_environment, targets, bond_sizes):
    sector = lax.axis_index("sector")
    shard = lax.axis_index("shard")
    blocks = lax.axis_size("sector")
    shards_n = lax.axis_size("shard")
    channels, _, rows, bond = left_environment.shape
    phys = wavefunction.shape[2] // bond
    col_parts = math.gcd(blocks, phys)
    row_parts = blocks // col_parts
    sub = rows // row_parts
    wide = (phys // col_parts) * bond
    own_row, own_col = sector // col_parts, sector % col_parts
    psi = wavefunction[0]

    e_own = masked(mask_left_kernel, channels, targets, bond_sizes, left_environment[:, 0])
    received = []
    for c in range(channels):
        f_own = right_environment[c, 0]
        f_parts = [f_own] + [exchange(f_own, "sector", k) for k in range(1, blocks)]
        kernel = functools.partial(mask_right_kernel, blocks=blocks, channel=c)
        f_masked, = masked(kernel, 1, targets, bond_sizes, *f_parts)
        e_pieces = gather_pieces(e_own[c])
        f_pieces = gather_pieces(f_masked)
        y = products(e_pieces, f_pieces, psi, row_parts, col_parts)
        received += [exchange(y[k], "sector", k) if k else y[k] for k in range(blocks)]

    totals = destination_sums(targets, received, blocks, 4)
    out = jnp.zeros((rows, shards_n * phys * bond), jnp.bfloat16)
    for j in range(blocks):
        total = exchange(totals[j], "sector", j) if j else totals[j]
        total = total.reshape(shards_n, sub, wide)
        row_at = (own_row ^ (j // col_parts)) * sub
        col_at = (own_col ^ (j % col_parts)) * wide
        for m in range(shards_n):
            part = exchange(total[m], "shard", m) if m else total[m]
            out = lax.dynamic_update_slice(out, part, (row_at, (shard ^ m) * phys * bond + col_at))
    return out[None]


def shards(wavefunction, left_environment, right_environment, targets, bond_sizes):
    group_index = lax.axis_index("sector")
    shard_index = lax.axis_index("shard")
    blocks = lax.axis_size("sector")
    channels = left_environment.shape[0]
    bond_dim = left_environment.shape[3]
    col_width = wavefunction.shape[2]
    positions = jnp.arange(bond_dim, dtype=jnp.int32)
    left_live = bond_sizes[0]
    right_live = bond_sizes[1]
    own_left = positions < left_live[group_index]
    own_right = positions < right_live[group_index]
    columns = shard_index * col_width + jnp.arange(col_width, dtype=jnp.int32)
    column_live = columns % bond_dim < right_live[group_index]
    psi_live = jnp.where(
        own_left[:, None] & column_live[None, :], wavefunction[0], jnp.zeros_like(wavefunction[0])
    )
    destination = targets[:, group_index]
    target_live = left_live[destination]
    env_rows = lax.all_gather(left_environment[:, 0], "shard", axis=1, tiled=True)
    row_ids = jnp.arange(env_rows.shape[1], dtype=jnp.int32)
    keep_mask = (row_ids[None, :, None] < target_live[:, None, None]) & own_left[None, None, :]
    env_live = jnp.where(keep_mask, env_rows, jnp.zeros_like(env_rows))
    halves = jnp.einsum(
        "crk,kw->crw", env_live, psi_live, preferred_element_type=jnp.float32
    ).astype(jnp.bfloat16)
    sector_ids = jnp.arange(blocks, dtype=jnp.int32)
    assign = (targets[:, None, :] == sector_ids[None, :, None]).astype(jnp.bfloat16)
    row_slabs = halves.reshape(channels, blocks, bond_dim // blocks, col_width)
    received = lax.all_to_all(row_slabs, "sector", split_axis=1, concat_axis=1, tiled=True)
    summed = jnp.einsum(
        "ctq,cqrw->ctrw", assign, received, preferred_element_type=jnp.float32
    ).astype(jnp.bfloat16)
    returned = lax.all_to_all(summed, "sector", split_axis=1, concat_axis=1, tiled=True)
    gathered_cols = returned.reshape(channels, bond_dim, col_width)
    arrived = lax.all_to_all(gathered_cols, "shard", split_axis=1, concat_axis=2, tiled=True)
    local_rows = arrived.shape[1]
    phys_count = arrived.shape[2] // bond_dim
    stacked = arrived.reshape(channels, local_rows, phys_count, bond_dim)
    env_rows = lax.all_gather(right_environment[:, 0], "shard", axis=1, tiled=True)
    row_ids = jnp.arange(env_rows.shape[1], dtype=jnp.int32)
    keep_mask = (row_ids < right_live[group_index])[None, :, None] & own_right[None, None, :]
    env_live = jnp.where(keep_mask, env_rows, jnp.zeros_like(env_rows))
    result = jnp.einsum("crpk,cnk->rpn", stacked, env_live, preferred_element_type=jnp.float32)
    return result.reshape(1, local_rows, phys_count * bond_dim).astype(jnp.bfloat16)


def fits(mesh, shape):
    blocks, shards_n = mesh.shape["sector"], mesh.shape["shard"]
    bond = shape[1]
    local = shape[2] // shards_n
    if local % bond or bond % shards_n or not (is_pow2(blocks) and is_pow2(shards_n)) or shards_n != 8:
        return False
    col_parts = math.gcd(blocks, local // bond)
    return (bond // shards_n) % (blocks // col_parts * 16) == 0


def solution(mesh):
    def whole(*arrays):
        quick = fits(mesh, arrays[0].shape)
        mapped = jax.shard_map(
            fast if quick else shards,
            mesh=mesh,
            in_specs=(
                P("sector", None, "shard"),
                P(None, "sector", "shard", None),
                P(None, "sector", "shard", None),
                P(),
                P(),
            ),
            out_specs=P("sector", "shard", None),
            check_vma=False,
        )
        return mapped(*arrays)

    return whole
```

profile of v0, /device:TPU:0, one launch (start us, length us, event | category | flops | bytes accessed | tf_op | source)
XLA Modules:
  0.0 214.0 jit_solution(8711267715566152308)
XLA Ops:
  1.0 3.0 %collective-permute-start.27 = (bf16[96,768]{1,0:T(8,128)(2,1)S(1)}, bf16[96,768]{1,0:T(8,128)(2,1)S(1)}, u32[]{:S(2)}, u32[]{:S(2)}) collective-permute-start(bf16[96,768]{1,0:T(8,128)(2,1)S(1)} %get-tuple-element.61.refs_0_), channel_id=1, source_target_pairs={{0,8},{8,0},{16,24},{24,16},{1,9},{9,1},{17,25},{25,17},{2,10},{10... | collective-permute-start | bytes 442376 | tf_op jit(solution)/shard_map/ppermute | solution.py:18
  9.4 2.6 %collective-permute-start.23 = (bf16[96,768]{1,0:T(8,128)(2,1)}, bf16[96,768]{1,0:T(8,128)(2,1)S(1)}, u32[]{:S(2)}, u32[]{:S(2)}) collective-permute-start(bf16[96,768]{1,0:T(8,128)(2,1)} %get-tuple-element.24.refs_0_), channel_id=1, source_target_pairs={{0,4},{1,5},{2,6},{3,7},{4,0},{5,1},{6,2},{7,3},{8,12},{9,13},{10,... | collective-permute-start | bytes 442376 | tf_op jit(solution)/shard_map/ppermute | solution.py:18
  17.3 2.6 %collective-permute-start.33 = (bf16[96,768]{1,0:T(8,128)(2,1)}, bf16[96,768]{1,0:T(8,128)(2,1)S(1)}, u32[]{:S(2)}, u32[]{:S(2)}) collective-permute-start(bf16[96,768]{1,0:T(8,128)(2,1)} %shard_map.57.refs_8_), channel_id=1, source_target_pairs={{0,4},{1,5},{2,6},{3,7},{4,0},{5,1},{6,2},{7,3},{8,12},{9,13},{10,... | collective-permute-start | bytes 442376 | tf_op jit(solution)/shard_map/ppermute | solution.py:18
  19.9 3.0 %collective-permute-done.23.refs_4_ = bf16[96,768]{1,0:T(8,128)(2,1)S(1)} collective-permute-done((bf16[96,768]{1,0:T(8,128)(2,1)}, bf16[96,768]{1,0:T(8,128)(2,1)S(1)}, u32[]{:S(2)}, u32[]{:S(2)}) %collective-permute-start.23) | collective-permute-done | bytes 147488 | tf_op jit(solution)/shard_map/ppermute | solution.py:18
  22.9 2.9 %collective-permute-start.35 = (bf16[96,768]{1,0:T(8,128)(2,1)}, bf16[96,768]{1,0:T(8,128)(2,1)S(1)}, u32[]{:S(2)}, u32[]{:S(2)}) collective-permute-start(bf16[96,768]{1,0:T(8,128)(2,1)} %shard_map.57.refs_8_), channel_id=1, source_target_pairs={{0,6},{1,7},{2,4},{3,5},{4,2},{5,3},{6,0},{7,1},{8,14},{9,15},{10,... | collective-permute-start | bytes 442376 | tf_op jit(solution)/shard_map/ppermute | solution.py:18
  26.4 9.1 %collective-permute-done.33.refs_12_ = bf16[96,768]{1,0:T(8,128)(2,1)S(1)} collective-permute-done((bf16[96,768]{1,0:T(8,128)(2,1)}, bf16[96,768]{1,0:T(8,128)(2,1)S(1)}, u32[]{:S(2)}, u32[]{:S(2)}) %collective-permute-start.33) | collective-permute-done | bytes 147488 | tf_op jit(solution)/shard_map/ppermute | solution.py:18
  43.3 7.7 %products.3 = (bf16[384,768]{1,0:T(8,128)(2,1)}, bf16[384,768]{1,0:T(8,128)(2,1)}, bf16[384,768]{1,0:T(8,128)(2,1)}, bf16[384,768]{1,0:T(8,128)(2,1)}) custom-call(bf16[96,768]{1,0:T(8,128)(2,1)} %get-tuple-element.24.refs_0_, bf16[96,768]{1,0:T(8,128)(2,1)} %copy-done.15, bf16[96,768]{1,0:T(8,128)(2,1)} %copy-done.12, bf16[96,768]{1,0:T(8,128)(2,1)} %copy-done.24, ...), custom_call_target="tpu_custom_call" | custom-call | tf_op jit(solution)/shard_map/products/pallas_call | solution.py:97
  61.5 3.8 %collective-permute-done.11.refs_10_ = bf16[96,768]{1,0:T(8,128)(2,1)S(1)} collective-permute-done((bf16[96,768]{1,0:T(8,128)(2,1)}, bf16[96,768]{1,0:T(8,128)(2,1)S(1)}, u32[]{:S(2)}, u32[]{:S(2)}) %collective-permute-start.11) | collective-permute-done | bytes 147488 | tf_op jit(solution)/shard_map/ppermute | solution.py:18
  65.3 6.4 %collective-permute-done.13.refs_12_ = bf16[96,768]{1,0:T(8,128)(2,1)S(1)} collective-permute-done((bf16[96,768]{1,0:T(8,128)(2,1)}, bf16[96,768]{1,0:T(8,128)(2,1)S(1)}, u32[]{:S(2)}, u32[]{:S(2)}) %collective-permute-start.13) | collective-permute-done | bytes 147488 | tf_op jit(solution)/shard_map/ppermute | solution.py:18
  76.1 7.6 %products.2 = (bf16[384,768]{1,0:T(8,128)(2,1)}, bf16[384,768]{1,0:T(8,128)(2,1)}, bf16[384,768]{1,0:T(8,128)(2,1)}, bf16[384,768]{1,0:T(8,128)(2,1)}) custom-call(bf16[96,768]{1,0:T(8,128)(2,1)} %get-tuple-element.19.refs_0_, bf16[96,768]{1,0:T(8,128)(2,1)} %copy-done.19, bf16[96,768]{1,0:T(8,128)(2,1)} %copy-done.10, bf16[96,768]{1,0:T(8,128)(2,1)} %copy-done.29, ...), custom_call_target="tpu_custom_call" | custom-call | tf_op jit(solution)/shard_map/products/pallas_call | solution.py:97
  87.2 15.2 %collective-permute-done.38.refs_6_ = bf16[384,768]{1,0:T(8,128)(2,1)S(1)} collective-permute-done((bf16[384,768]{1,0:T(8,128)(2,1)}, bf16[384,768]{1,0:T(8,128)(2,1)S(1)}, u32[]{:S(2)}, u32[]{:S(2)}) %collective-permute-start.38) | collective-permute-done | bytes 589856 | tf_op jit(solution)/shard_map/ppermute | solution.py:18
  103.9 23.1 %collective-permute-done.18.refs_2_ = bf16[384,768]{1,0:T(8,128)(2,1)S(1)} collective-permute-done((bf16[384,768]{1,0:T(8,128)(2,1)}, bf16[384,768]{1,0:T(8,128)(2,1)S(1)}, u32[]{:S(2)}, u32[]{:S(2)}) %collective-permute-start.18) | collective-permute-done | bytes 589856 | tf_op jit(solution)/shard_map/ppermute | solution.py:18
  128.0 5.0 %destination_sums.1 = (bf16[384,768]{1,0:T(8,128)(2,1)}, bf16[384,768]{1,0:T(8,128)(2,1)}, bf16[384,768]{1,0:T(8,128)(2,1)}, bf16[384,768]{1,0:T(8,128)(2,1)}) custom-call(s32[2,4]{1,0:T(2,128)} %targets.7, bf16[384,768]{1,0:T(8,128)(2,1)} %get-tuple-element.20.refs_0_, bf16[384,768]{1,0:T(8,128)(2,1)} %copy-done.4, bf16[384,768]{1,0:T(8,128)(2,1)} %copy-done.5, ...), custom_call_target="tpu_custom_call" | custom-call | tf_op jit(solution)/shard_map/destination_sums/pallas_call | solution.py:122
  134.4 2.6 %collective-permute-start.41 = (bf16[48,768]{1,0:T(8,128)(2,1)S(1)}, bf16[48,768]{1,0:T(8,128)(2,1)S(1)}, u32[]{:S(2)}, u32[]{:S(2)}) collective-permute-start(bf16[48,768]{1,0:T(8,128)(2,1)S(1)} %get-tuple-element.59), channel_id=1, source_target_pairs={{0,2},{1,3},{2,0},{3,1},{4,6},{5,7},{6,4},{7,5},{8,10},{9,11},{10,... | collective-permute-start | bytes 221192 | tf_op jit(solution)/shard_map/ppermute | solution.py:18
  146.7 3.8 %collective-permute-done.44 = bf16[48,768]{1,0:T(8,128)(2,1)S(1)} collective-permute-done((bf16[48,768]{1,0:T(8,128)(2,1)S(1)}, bf16[48,768]{1,0:T(8,128)(2,1)S(1)}, u32[]{:S(2)}, u32[]{:S(2)}) %collective-permute-start.44) | collective-permute-done | bytes 73760 | tf_op jit(solution)/shard_map/ppermute | solution.py:18
  152.1 8.6 %collective-permute-done.47 = bf16[384,768]{1,0:T(8,128)(2,1)S(1)} collective-permute-done((bf16[384,768]{1,0:T(8,128)(2,1)S(1)}, bf16[384,768]{1,0:T(8,128)(2,1)S(1)}, u32[]{:S(2)}, u32[]{:S(2)}) %collective-permute-start.47) | collective-permute-done | bytes 589856 | tf_op jit(solution)/shard_map/ppermute | solution.py:18
  162.7 9.3 %collective-permute-done.55 = bf16[384,768]{1,0:T(8,128)(2,1)S(1)} collective-permute-done((bf16[384,768]{1,0:T(8,128)(2,1)S(1)}, bf16[384,768]{1,0:T(8,128)(2,1)S(1)}, u32[]{:S(2)}, u32[]{:S(2)}) %collective-permute-start.55) | collective-permute-done | bytes 589856 | tf_op jit(solution)/shard_map/ppermute | solution.py:18
  175.6 2.9 %collective-permute-start.54 = (bf16[48,768]{1,0:T(8,128)(2,1)S(1)}, bf16[48,768]{1,0:T(8,128)(2,1)S(1)}, u32[]{:S(2)}, u32[]{:S(2)}) collective-permute-start(bf16[48,768]{1,0:T(8,128)(2,1)S(1)} %get-tuple-element.47), channel_id=1, source_target_pairs={{0,7},{1,6},{2,5},{3,4},{4,3},{5,2},{6,1},{7,0},{8,15},{9,14},{10,... | collective-permute-start | bytes 221192 | tf_op jit(solution)/shard_map/ppermute | solution.py:18
  178.7 3.9 %collective-permute-done.51 = bf16[48,768]{1,0:T(8,128)(2,1)S(1)} collective-permute-done((bf16[48,768]{1,0:T(8,128)(2,1)S(1)}, bf16[48,768]{1,0:T(8,128)(2,1)S(1)}, u32[]{:S(2)}, u32[]{:S(2)}) %collective-permute-start.51) | collective-permute-done | bytes 73760 | tf_op jit(solution)/shard_map/ppermute | solution.py:18
  183.2 4.0 %collective-permute-start.59 = (bf16[48,768]{1,0:T(8,128)(2,1)S(1)}, bf16[48,768]{1,0:T(8,128)(2,1)S(1)}, u32[]{:S(2)}, u32[]{:S(2)}) collective-permute-start(bf16[48,768]{1,0:T(8,128)(2,1)S(1)} %get-tuple-element.43), channel_id=1, source_target_pairs={{0,4},{1,5},{2,6},{3,7},{4,0},{5,1},{6,2},{7,3},{8,12},{9,13},{10,... | collective-permute-start | bytes 221192 | tf_op jit(solution)/shard_map/ppermute | solution.py:18
  192.1 4.5 %collective-permute-done.59 = bf16[48,768]{1,0:T(8,128)(2,1)S(1)} collective-permute-done((bf16[48,768]{1,0:T(8,128)(2,1)S(1)}, bf16[48,768]{1,0:T(8,128)(2,1)S(1)}, u32[]{:S(2)}, u32[]{:S(2)}) %collective-permute-start.59) | collective-permute-done | bytes 73760 | tf_op jit(solution)/shard_map/ppermute | solution.py:18
  197.7 3.0 %collective-permute-start.67 = (bf16[48,768]{1,0:T(8,128)(2,1)S(1)}, bf16[48,768]{1,0:T(8,128)(2,1)S(1)}, u32[]{:S(2)}, u32[]{:S(2)}) collective-permute-start(bf16[48,768]{1,0:T(8,128)(2,1)S(1)} %get-tuple-element.36), channel_id=1, source_target_pairs={{0,4},{1,5},{2,6},{3,7},{4,0},{5,1},{6,2},{7,3},{8,12},{9,13},{10,... | collective-permute-start | bytes 221192 | tf_op jit(solution)/shard_map/ppermute | solution.py:18
  205.3 3.1 %collective-permute-done.67 = bf16[48,768]{1,0:T(8,128)(2,1)S(1)} collective-permute-done((bf16[48,768]{1,0:T(8,128)(2,1)S(1)}, bf16[48,768]{1,0:T(8,128)(2,1)S(1)}, u32[]{:S(2)}, u32[]{:S(2)}) %collective-permute-start.67) | collective-permute-done | bytes 73760 | tf_op jit(solution)/shard_map/ppermute | solution.py:18
  208.4 3.5 %collective-permute-done.68 = bf16[48,768]{1,0:T(8,128)(2,1)S(1)} collective-permute-done((bf16[48,768]{1,0:T(8,128)(2,1)S(1)}, bf16[48,768]{1,0:T(8,128)(2,1)S(1)}, u32[]{:S(2)}, u32[]{:S(2)}) %collective-permute-start.68) | collective-permute-done | bytes 73760 | tf_op jit(solution)/shard_map/ppermute | solution.py:18
  (254 shorter events, 72.0 us)
Async XLA Ops:
  9.4 13.5 %collective-permute-start.23 = (bf16[96,768]{1,0:T(8,128)(2,1)}, bf16[96,768]{1,0:T(8,128)(2,1)S(1)}, u32[]{:S(2)}, u32[]{:S(2)}) collective-permute-start(bf16[96,768]{1,0:T(8,128)(2,1)} %get-tuple-element.24.refs_0_), channel_id=1, source_target_pairs={{0,4},{1,5},{2,6},{3,7},{4,0},{5,1},{6,2},{7,3},{8,12},{9,13},{10,... | collective-permute-start | bytes 442376 | tf_op jit(solution)/shard_map/ppermute | solution.py:18
  12.0 13.8 %collective-permute-start.25 = (bf16[96,768]{1,0:T(8,128)(2,1)}, bf16[96,768]{1,0:T(8,128)(2,1)S(1)}, u32[]{:S(2)}, u32[]{:S(2)}) collective-permute-start(bf16[96,768]{1,0:T(8,128)(2,1)} %get-tuple-element.24.refs_0_), channel_id=1, source_target_pairs={{0,6},{1,7},{2,4},{3,5},{4,2},{5,3},{6,0},{7,1},{8,14},{9,15},{10,... | collective-permute-start | bytes 442376 | tf_op jit(solution)/shard_map/ppermute | solution.py:18
  12.5 13.3 %collective-permute-start.20 = (bf16[96,768]{1,0:T(8,128)(2,1)}, bf16[96,768]{1,0:T(8,128)(2,1)S(1)}, u32[]{:S(2)}, u32[]{:S(2)}) collective-permute-start(bf16[96,768]{1,0:T(8,128)(2,1)} %get-tuple-element.24.refs_0_), channel_id=1, source_target_pairs={{0,1},{1,0},{2,3},{3,2},{4,5},{5,4},{6,7},{7,6},{8,9},{9,8},{10,11... | collective-permute-start | bytes 442376 | tf_op jit(solution)/shard_map/ppermute | solution.py:18
  17.3 18.2 %collective-permute-start.33 = (bf16[96,768]{1,0:T(8,128)(2,1)}, bf16[96,768]{1,0:T(8,128)(2,1)S(1)}, u32[]{:S(2)}, u32[]{:S(2)}) collective-permute-start(bf16[96,768]{1,0:T(8,128)(2,1)} %shard_map.57.refs_8_), channel_id=1, source_target_pairs={{0,4},{1,5},{2,6},{3,7},{4,0},{5,1},{6,2},{7,3},{8,12},{9,13},{10,... | collective-permute-start | bytes 442376 | tf_op jit(solution)/shard_map/ppermute | solution.py:18
  22.9 12.6 %collective-permute-start.35 = (bf16[96,768]{1,0:T(8,128)(2,1)}, bf16[96,768]{1,0:T(8,128)(2,1)S(1)}, u32[]{:S(2)}, u32[]{:S(2)}) collective-permute-start(bf16[96,768]{1,0:T(8,128)(2,1)} %shard_map.57.refs_8_), channel_id=1, source_target_pairs={{0,6},{1,7},{2,4},{3,5},{4,2},{5,3},{6,0},{7,1},{8,14},{9,15},{10,... | collective-permute-start | bytes 442376 | tf_op jit(solution)/shard_map/ppermute | solution.py:18
  36.6 14.3 %collective-permute-start.7 = (bf16[96,768]{1,0:T(8,128)(2,1)S(1)}, bf16[96,768]{1,0:T(8,128)(2,1)S(1)}, u32[]{:S(2)}, u32[]{:S(2)}) collective-permute-start(bf16[96,768]{1,0:T(8,128)(2,1)S(1)} %get-tuple-element.62.refs_0_), channel_id=1, source_target_pairs={{0,8},{8,0},{16,24},{24,16},{1,9},{9,1},{17,25},{25,17},{2,10},{10... | collective-permute-start | bytes 442376 | tf_op jit(solution)/shard_map/ppermute | solution.py:18
  38.1 14.4 %collective-permute-start.8 = (bf16[96,768]{1,0:T(8,128)(2,1)S(1)}, bf16[96,768]{1,0:T(8,128)(2,1)S(1)}, u32[]{:S(2)}, u32[]{:S(2)}) collective-permute-start(bf16[96,768]{1,0:T(8,128)(2,1)S(1)} %get-tuple-element.62.refs_0_), channel_id=1, source_target_pairs={{0,16},{8,24},{16,0},{24,8},{1,17},{9,25},{17,1},{25,9},{2,18},{10... | collective-permute-start | bytes 442376 | tf_op jit(solution)/shard_map/ppermute | solution.py:18
  39.6 14.6 %collective-permute-start.9 = (bf16[96,768]{1,0:T(8,128)(2,1)S(1)}, bf16[96,768]{1,0:T(8,128)(2,1)S(1)}, u32[]{:S(2)}, u32[]{:S(2)}) collective-permute-start(bf16[96,768]{1,0:T(8,128)(2,1)S(1)} %get-tuple-element.62.refs_0_), channel_id=1, source_target_pairs={{0,24},{8,16},{16,8},{24,0},{1,25},{9,17},{17,9},{25,1},{2,26},{10... | collective-permute-start | bytes 442376 | tf_op jit(solution)/shard_map/ppermute | solution.py:18
  40.1 16.9 %collective-permute-start.1 = (bf16[96,768]{1,0:T(8,128)(2,1)}, bf16[96,768]{1,0:T(8,128)(2,1)S(1)}, u32[]{:S(2)}, u32[]{:S(2)}) collective-permute-start(bf16[96,768]{1,0:T(8,128)(2,1)} %get-tuple-element.19.refs_0_), channel_id=1, source_target_pairs={{0,2},{1,3},{2,0},{3,1},{4,6},{5,7},{6,4},{7,5},{8,10},{9,11},{10,... | collective-permute-start | bytes 442376 | tf_op jit(solution)/shard_map/ppermute | solution.py:18
  41.8 15.7 %collective-permute-start.3 = (bf16[96,768]{1,0:T(8,128)(2,1)}, bf16[96,768]{1,0:T(8,128)(2,1)S(1)}, u32[]{:S(2)}, u32[]{:S(2)}) collective-permute-start(bf16[96,768]{1,0:T(8,128)(2,1)} %get-tuple-element.19.refs_0_), channel_id=1, source_target_pairs={{0,4},{1,5},{2,6},{3,7},{4,0},{5,1},{6,2},{7,3},{8,12},{9,13},{10,... | collective-permute-start | bytes 442376 | tf_op jit(solution)/shard_map/ppermute | solution.py:18
  51.0 35.7 %collective-permute-start.37 = (bf16[384,768]{1,0:T(8,128)(2,1)}, bf16[384,768]{1,0:T(8,128)(2,1)S(1)}, u32[]{:S(2)}, u32[]{:S(2)}) collective-permute-start(bf16[384,768]{1,0:T(8,128)(2,1)} %get-tuple-element.26), channel_id=1, source_target_pairs={{0,8},{8,0},{16,24},{24,16},{1,9},{9,1},{17,25},{25,17},{2,10},{10... | collective-permute-start | bytes 1769480 | tf_op jit(solution)/shard_map/ppermute | solution.py:18
  57.6 14.2 %collective-permute-start.13 = (bf16[96,768]{1,0:T(8,128)(2,1)}, bf16[96,768]{1,0:T(8,128)(2,1)S(1)}, u32[]{:S(2)}, u32[]{:S(2)}) collective-permute-start(bf16[96,768]{1,0:T(8,128)(2,1)} %shard_map.56.refs_8_), channel_id=1, source_target_pairs={{0,4},{1,5},{2,6},{3,7},{4,0},{5,1},{6,2},{7,3},{8,12},{9,13},{10,... | collective-permute-start | bytes 442376 | tf_op jit(solution)/shard_map/ppermute | solution.py:18
  73.3 29.1 %collective-permute-start.38 = (bf16[384,768]{1,0:T(8,128)(2,1)}, bf16[384,768]{1,0:T(8,128)(2,1)S(1)}, u32[]{:S(2)}, u32[]{:S(2)}) collective-permute-start(bf16[384,768]{1,0:T(8,128)(2,1)} %get-tuple-element.27), channel_id=1, source_target_pairs={{0,16},{8,24},{16,0},{24,8},{1,17},{9,25},{17,1},{25,9},{2,18},{10... | collective-permute-start | bytes 1769480 | tf_op jit(solution)/shard_map/ppermute | solution.py:18
  74.8 27.5 %collective-permute-start.39 = (bf16[384,768]{1,0:T(8,128)(2,1)}, bf16[384,768]{1,0:T(8,128)(2,1)S(1)}, u32[]{:S(2)}, u32[]{:S(2)}) collective-permute-start(bf16[384,768]{1,0:T(8,128)(2,1)} %get-tuple-element.28), channel_id=1, source_target_pairs={{0,24},{8,16},{16,8},{24,0},{1,25},{9,17},{17,9},{25,1},{2,26},{10... | collective-permute-start | bytes 1769480 | tf_op jit(solution)/shard_map/ppermute | solution.py:18
  83.7 20.2 %collective-permute-start.17 = (bf16[384,768]{1,0:T(8,128)(2,1)}, bf16[384,768]{1,0:T(8,128)(2,1)S(1)}, u32[]{:S(2)}, u32[]{:S(2)}) collective-permute-start(bf16[384,768]{1,0:T(8,128)(2,1)} %get-tuple-element.21), channel_id=1, source_target_pairs={{0,8},{8,0},{16,24},{24,16},{1,9},{9,1},{17,25},{25,17},{2,10},{10... | collective-permute-start | bytes 1769480 | tf_op jit(solution)/shard_map/ppermute | solution.py:18
  85.2 41.8 %collective-permute-start.18 = (bf16[384,768]{1,0:T(8,128)(2,1)}, bf16[384,768]{1,0:T(8,128)(2,1)S(1)}, u32[]{:S(2)}, u32[]{:S(2)}) collective-permute-start(bf16[384,768]{1,0:T(8,128)(2,1)} %get-tuple-element.22), channel_id=1, source_target_pairs={{0,16},{8,24},{16,0},{24,8},{1,17},{9,25},{17,1},{25,9},{2,18},{10... | collective-permute-start | bytes 1769480 | tf_op jit(solution)/shard_map/ppermute | solution.py:18
  86.7 40.3 %collective-permute-start.19 = (bf16[384,768]{1,0:T(8,128)(2,1)}, bf16[384,768]{1,0:T(8,128)(2,1)S(1)}, u32[]{:S(2)}, u32[]{:S(2)}) collective-permute-start(bf16[384,768]{1,0:T(8,128)(2,1)} %get-tuple-element.23), channel_id=1, source_target_pairs={{0,24},{8,16},{16,8},{24,0},{1,25},{9,17},{17,9},{25,1},{2,26},{10... | collective-permute-start | bytes 1769480 | tf_op jit(solution)/shard_map/ppermute | solution.py:18
  144.5 16.3 %collective-permute-start.47 = (bf16[384,768]{1,0:T(8,128)(2,1)S(1)}, bf16[384,768]{1,0:T(8,128)(2,1)S(1)}, u32[]{:S(2)}, u32[]{:S(2)}) collective-permute-start(bf16[384,768]{1,0:T(8,128)(2,1)S(1)} %copy-done.45), channel_id=1, source_target_pairs={{0,8},{8,0},{16,24},{24,16},{1,9},{9,1},{17,25},{25,17},{2,10},{10... | collective-permute-start | bytes 1769480 | tf_op jit(solution)/shard_map/ppermute | solution.py:18
  145.1 26.9 %collective-permute-start.55 = (bf16[384,768]{1,0:T(8,128)(2,1)S(1)}, bf16[384,768]{1,0:T(8,128)(2,1)S(1)}, u32[]{:S(2)}, u32[]{:S(2)}) collective-permute-start(bf16[384,768]{1,0:T(8,128)(2,1)S(1)} %copy-done.44), channel_id=1, source_target_pairs={{0,16},{8,24},{16,0},{24,8},{1,17},{9,25},{17,1},{25,9},{2,18},{10... | collective-permute-start | bytes 1769480 | tf_op jit(solution)/shard_map/ppermute | solution.py:18
  150.6 23.0 %collective-permute-start.63 = (bf16[384,768]{1,0:T(8,128)(2,1)S(1)}, bf16[384,768]{1,0:T(8,128)(2,1)S(1)}, u32[]{:S(2)}, u32[]{:S(2)}) collective-permute-start(bf16[384,768]{1,0:T(8,128)(2,1)S(1)} %copy-done.43), channel_id=1, source_target_pairs={{0,24},{8,16},{16,8},{24,0},{1,25},{9,17},{17,9},{25,1},{2,26},{10... | collective-permute-start | bytes 1769480 | tf_op jit(solution)/shard_map/ppermute | solution.py:18
  160.8 12.8 %collective-permute-start.48 = (bf16[48,768]{1,0:T(8,128)(2,1)S(1)}, bf16[48,768]{1,0:T(8,128)(2,1)S(1)}, u32[]{:S(2)}, u32[]{:S(2)}) collective-permute-start(bf16[48,768]{1,0:T(8,128)(2,1)S(1)} %get-tuple-element.53), channel_id=1, source_target_pairs={{0,1},{1,0},{2,3},{3,2},{4,5},{5,4},{6,7},{7,6},{8,9},{9,8},{10,11... | collective-permute-start | bytes 221192 | tf_op jit(solution)/shard_map/ppermute | solution.py:18
  160.9 14.7 %collective-permute-start.49 = (bf16[48,768]{1,0:T(8,128)(2,1)S(1)}, bf16[48,768]{1,0:T(8,128)(2,1)S(1)}, u32[]{:S(2)}, u32[]{:S(2)}) collective-permute-start(bf16[48,768]{1,0:T(8,128)(2,1)S(1)} %get-tuple-element.52), channel_id=1, source_target_pairs={{0,2},{1,3},{2,0},{3,1},{4,6},{5,7},{6,4},{7,5},{8,10},{9,11},{10,... | collective-permute-start | bytes 221192 | tf_op jit(solution)/shard_map/ppermute | solution.py:18
  161.0 17.6 %collective-permute-start.50 = (bf16[48,768]{1,0:T(8,128)(2,1)S(1)}, bf16[48,768]{1,0:T(8,128)(2,1)S(1)}, u32[]{:S(2)}, u32[]{:S(2)}) collective-permute-start(bf16[48,768]{1,0:T(8,128)(2,1)S(1)} %get-tuple-element.51), channel_id=1, source_target_pairs={{0,3},{1,2},{2,1},{3,0},{4,7},{5,6},{6,5},{7,4},{8,11},{9,10},{10,... | collective-permute-start | bytes 221192 | tf_op jit(solution)/shard_map/ppermute | solution.py:18
  183.2 13.4 %collective-permute-start.59 = (bf16[48,768]{1,0:T(8,128)(2,1)S(1)}, bf16[48,768]{1,0:T(8,128)(2,1)S(1)}, u32[]{:S(2)}, u32[]{:S(2)}) collective-permute-start(bf16[48,768]{1,0:T(8,128)(2,1)S(1)} %get-tuple-element.43), channel_id=1, source_target_pairs={{0,4},{1,5},{2,6},{3,7},{4,0},{5,1},{6,2},{7,3},{8,12},{9,13},{10,... | collective-permute-start | bytes 221192 | tf_op jit(solution)/shard_map/ppermute | solution.py:18
  (93 other events, 867.6 us)
where the time goes:
time: 215 us; the launch traced here: 214 us
  waiting for transfers between devices  102 us (47%)
  starting transfers between devices  75.7 us (35%)
  Pallas kernels  26 us (12%)
  local copies, waits for them, and re-layouts  9.5 us (4%)
    ppermute x71, waiting for transfers between devices, exchange(): return lax.ppermute(x, axis, [(a, a ^ offset) for a in range(size)])  102 us
    ppermute x71, starting transfers between devices, exchange(): return lax.ppermute(x, axis, [(a, a ^ offset) for a in range(size)])  75.7 us
    pallas_call x2, Pallas kernels, products(): pl.pallas_call(functools.partial(products_kernel, shards_n=shards_n, row_...  15.2 us
    pallas_call x3, Pallas kernels, masked(): pl.pallas_call(kernel, out_shape=[jax.ShapeDtypeStruct((rows, bond), jnp....  5.72 us
    unnamed x92, local copies, waits for them, and re-layouts  5.1 us
    pallas_call x1, Pallas kernels, destination_sums(): pl.pallas_call(functools.partial(sum_kernel, blocks=blocks), grid=(steps,...  5.04 us
  transfers between devices with their start and end apart: 71, of which 19 were waited for; matrix products, arithmetic and copies ran while one was open for 1% of the time, Pallas kernels for 10%

commit v1 on v0

v1 whole, which is shorter than its diff:
```python
import functools

import jax
import jax.numpy as jnp
from jax import lax
from jax.experimental import pallas as pl
from jax.experimental.pallas import tpu as pltpu
from jax.sharding import PartitionSpec as P


def is_pow2(n):
    return n & (n - 1) == 0


def exchange(x, axis, offset):
    size = lax.axis_size(axis)
    return lax.ppermute(x, axis, [(a, a ^ offset) for a in range(size)])


def gather_pieces(piece):
    pieces = []
    for m in range(0, lax.axis_size("shard"), 2):
        near = exchange(piece, "shard", m) if m else piece
        pieces += [near, exchange(near, "shard", 1)]
    return pieces


def live_mask(shape, rows_live, cols_live, row_start):
    row = lax.broadcasted_iota(jnp.int32, shape, 0) + row_start
    col = lax.broadcasted_iota(jnp.int32, shape, 1)
    return (row < rows_live) & (col < cols_live)


def mask_left(targets, sizes, channel, block):
    sector, shard = lax.axis_index("sector"), lax.axis_index("shard")
    rows = block.shape[0]
    keep = live_mask(block.shape, sizes[0, targets[channel, sector]], sizes[0, sector], shard * rows)
    return jnp.where(keep, block, 0).astype(block.dtype)


def prepare_kernel(targets, sizes, e_ref, f_ref, left, *rights):
    left[...] = mask_left(targets, sizes, 0, e_ref[0])
    for c, right in enumerate(rights):
        right[...] = f_ref[c]


def mask_right_kernel(targets, sizes, *refs, blocks, channel):
    sources, out, held = refs[:blocks], refs[-2], refs[-1]
    sector, shard = lax.axis_index("sector"), lax.axis_index("shard")
    target = targets[channel, sector]
    for k in range(blocks):
        @pl.when(target == sector ^ k)
        def _(k=k):
            held[...] = sources[k][...]
    live = sizes[1, target]
    keep = live_mask(held.shape, live, jnp.minimum(live, sizes[1, sector]), shard * held.shape[0])
    right = jnp.where(keep, held[...], 0).astype(held.dtype)
    if channel:
        out[0] = mask_left(targets, sizes, channel, refs[blocks][channel])
        out[1] = right
    else:
        out[...] = right


def prepare(targets, sizes, e_own, f_own):
    channels = f_own.shape[0]
    full, scalars = pl.BlockSpec(memory_space=pltpu.VMEM), pl.BlockSpec(memory_space=pltpu.SMEM)
    return pl.pallas_call(
        prepare_kernel,
        out_shape=[jax.ShapeDtypeStruct(e_own.shape[1:], jnp.bfloat16)] * (channels + 1),
        in_specs=[scalars, scalars, full, full],
        out_specs=[full] * (channels + 1),
        name="prepare",
    )(targets, sizes, e_own, f_own)


def masked_right(targets, sizes, f_parts, e_own, channel):
    rows, bond = e_own.shape[1:]
    full, scalars = pl.BlockSpec(memory_space=pltpu.VMEM), pl.BlockSpec(memory_space=pltpu.SMEM)
    extra = [e_own] * bool(channel)
    return pl.pallas_call(
        functools.partial(mask_right_kernel, blocks=len(f_parts), channel=channel),
        out_shape=jax.ShapeDtypeStruct((2, rows, bond) if channel else (rows, bond), jnp.bfloat16),
        in_specs=[scalars] * 2 + [full] * len(f_parts) + [full] * len(extra),
        out_specs=full,
        scratch_shapes=[pltpu.VMEM((rows, bond), jnp.bfloat16)],
        name="mask_right",
    )(targets, sizes, *f_parts, *extra)


def shard_chunks(shards_n):
    first = list(range(2, 2 + shards_n // 2))
    return first, [m for m in range(shards_n) if m not in first]


def products_kernel(*refs, shards_n, row_parts, col_parts, parts):
    y_refs = refs[-2 - row_parts * col_parts * parts:-2]
    pieces, psi_ref = refs[:-len(y_refs) - 3], refs[-len(y_refs) - 3]
    if len(pieces) == shards_n:
        pieces = [ref.at[n] for n in range(2) for ref in pieces]
    e_refs, f_refs = pieces[:shards_n], pieces[shards_n:]
    left_ref, right_ref = refs[-2:]
    rows, bond = e_refs[0].shape
    sub = rows // row_parts
    block = shards_n * sub
    sector, shard = lax.axis_index("sector"), lax.axis_index("shard")
    own_row, own_col = sector // col_parts, sector % col_parts
    for m in range(shards_n):
        right_ref[pl.ds(pl.multiple_of((shard ^ m) * rows, 16), rows), :] = f_refs[m][...]
    for n, m in enumerate(sum(shard_chunks(shards_n), [])):
        for h in range(row_parts):
            at = pl.multiple_of((own_row ^ h) * sub, 16)
            left_ref[h * block + n * sub:h * block + (n + 1) * sub, :] = e_refs[m][pl.ds(at, sub), :]
    for g in range(col_parts):
        at = pl.multiple_of((own_col ^ g) * bond, 128)
        half = jnp.dot(left_ref[...], psi_ref[:, pl.ds(at, bond)], preferred_element_type=jnp.float32)
        y = lax.dot_general(half.astype(jnp.bfloat16), right_ref[...], (((1,), (1,)), ((), ())),
                            preferred_element_type=jnp.float32).astype(jnp.bfloat16)
        size = block // parts
        for h in range(row_parts):
            for u in range(parts):
                start = h * block + u * size
                y_refs[(h * col_parts + g) * parts + u][...] = y[start:start + size]


def products(pieces, psi, shards_n, row_parts, col_parts, parts):
    rows, bond = pieces[0].shape[-2:]
    blocks = row_parts * col_parts
    full = pl.BlockSpec(memory_space=pltpu.VMEM)
    out = jax.ShapeDtypeStruct((shards_n * rows // row_parts // parts, bond), jnp.bfloat16)
    made = pl.pallas_call(
        functools.partial(products_kernel, shards_n=shards_n, row_parts=row_parts, col_parts=col_parts,
                          parts=parts),
        out_shape=[out] * (blocks * parts),
        in_specs=[full] * (len(pieces) + 1),
        out_specs=[full] * (blocks * parts),
        scratch_shapes=[pltpu.VMEM((bond, bond), jnp.bfloat16)] * 2,
        name="products",
    )(*pieces, psi)
    return [made[k * parts:(k + 1) * parts] for k in range(blocks)]


def sum_kernel(targets, *refs, blocks, own_n, steps):
    sources, outs = refs[:-own_n - blocks], refs[-own_n - blocks:-own_n - 1]
    own, acc = refs[-own_n - 1:-1], refs[-1]
    sub = own[0].shape[0]
    sector = lax.axis_index("sector")
    acc[...] = jnp.zeros_like(acc)
    for n, ref in enumerate(sources):
        j = targets[n // blocks, sector ^ (n % blocks)] ^ sector
        acc[j] = acc[j] + ref[...].astype(jnp.float32)
    for j in range(1, blocks):
        outs[j - 1][...] = acc[j].astype(jnp.bfloat16)
    per = own_n // steps
    for step in range(steps):
        @pl.when(pl.program_id(0) == step)
        def _(step=step):
            for n in range(per):
                own[step * per + n][...] = acc[0, n * sub:(n + 1) * sub].astype(jnp.bfloat16)


def destination_sums(targets, sources, starts, blocks, rows, own_n, steps):
    width = sources[0].shape[1]
    step, sub = rows // steps, rows // own_n
    specs = [pl.BlockSpec((step, width), lambda n, at=at // step: (n + at, 0)) for at in starts]
    return pl.pallas_call(
        functools.partial(sum_kernel, blocks=blocks, own_n=own_n, steps=steps),
        grid=(steps,),
        out_shape=[jax.ShapeDtypeStruct((rows, width), jnp.bfloat16)] * (blocks - 1)
        + [jax.ShapeDtypeStruct((sub, width), jnp.bfloat16)] * own_n,
        in_specs=[pl.BlockSpec(memory_space=pltpu.SMEM)] + specs,
        out_specs=[pl.BlockSpec((step, width), lambda n: (n, 0))] * (blocks - 1)
        + [pl.BlockSpec((sub, width), lambda n: (0, 0))] * own_n,
        scratch_shapes=[pltpu.VMEM((blocks, step, width), jnp.float32)],
        name="destination_sums",
    )(targets, *sources)


def fast(*arrays):
    return apply_blocks(*arrays)


def apply_blocks(wavefunction, left_environment, right_environment, targets, bond_sizes):
    sector = lax.axis_index("sector")
    shard = lax.axis_index("shard")
    blocks = lax.axis_size("sector")
    shards_n = lax.axis_size("shard")
    channels, _, rows, bond = left_environment.shape
    col_parts = wavefunction.shape[2] // bond
    row_parts = blocks // col_parts
    sub = rows // row_parts
    own_row, own_col = sector // col_parts, sector % col_parts
    psi = wavefunction[0]

    received = []
    e_own = left_environment[:, 0]
    left, *f_own = prepare(targets, bond_sizes, e_own, right_environment[:, 0])
    for c in range(channels):
        f_parts = [f_own[c]] + [exchange(f_own[c], "sector", k) for k in range(1, blocks)]
        right = masked_right(targets, bond_sizes, f_parts, e_own, c)
        if c:
            pieces = gather_pieces(right)
        else:
            pieces = gather_pieces(left) + gather_pieces(right)
        y = products(pieces, psi, shards_n, row_parts, col_parts, 2 if c + 1 == channels else 1)
        received.append([
            [exchange(part, "sector", k) if k else part for part in y[k]]
            for k in range(blocks)])

    placed = []
    for u, chunk in enumerate(shard_chunks(shards_n)):
        chunk_rows = len(chunk) * sub
        parts = [parts for channel in received for parts in channel]
        totals = destination_sums(
            targets, [p[u % len(p)] for p in parts], [0 if len(p) > 1 else u * chunk_rows for p in parts],
            blocks, chunk_rows, len(chunk), 2)
        for j in range(blocks):
            row_at = (own_row ^ (j // col_parts)) * sub
            col_at = (own_col ^ (j % col_parts)) * bond
            if j:
                total = exchange(totals[j - 1], "sector", j).reshape(len(chunk), sub, bond)
            for n, m in enumerate(chunk):
                part = total[n] if j else totals[blocks - 1 + n]
                part = exchange(part, "shard", m) if m else part
                placed.append((part, row_at, (shard ^ m) * col_parts * bond + col_at))
    out = jnp.zeros((rows, shards_n * col_parts * bond), jnp.bfloat16)
    for part, row_at, col_at in placed:
        out = lax.dynamic_update_slice(out, part, (row_at, col_at))
    return out[None]


def shards(wavefunction, left_environment, right_environment, targets, bond_sizes):
    group_index = lax.axis_index("sector")
    shard_index = lax.axis_index("shard")
    blocks = lax.axis_size("sector")
    channels = left_environment.shape[0]
    bond_dim = left_environment.shape[3]
    col_width = wavefunction.shape[2]
    positions = jnp.arange(bond_dim, dtype=jnp.int32)
    left_live = bond_sizes[0]
    right_live = bond_sizes[1]
    own_left = positions < left_live[group_index]
    own_right = positions < right_live[group_index]
    columns = shard_index * col_width + jnp.arange(col_width, dtype=jnp.int32)
    column_live = columns % bond_dim < right_live[group_index]
    psi_live = jnp.where(
        own_left[:, None] & column_live[None, :], wavefunction[0], jnp.zeros_like(wavefunction[0])
    )
    destination = targets[:, group_index]
    target_live = left_live[destination]
    env_rows = lax.all_gather(left_environment[:, 0], "shard", axis=1, tiled=True)
    row_ids = jnp.arange(env_rows.shape[1], dtype=jnp.int32)
    keep_mask = (row_ids[None, :, None] < target_live[:, None, None]) & own_left[None, None, :]
    env_live = jnp.where(keep_mask, env_rows, jnp.zeros_like(env_rows))
    halves = jnp.einsum(
        "crk,kw->crw", env_live, psi_live, preferred_element_type=jnp.float32
    ).astype(jnp.bfloat16)
    sector_ids = jnp.arange(blocks, dtype=jnp.int32)
    assign = (targets[:, None, :] == sector_ids[None, :, None]).astype(jnp.bfloat16)
    row_slabs = halves.reshape(channels, blocks, bond_dim // blocks, col_width)
    received = lax.all_to_all(row_slabs, "sector", split_axis=1, concat_axis=1, tiled=True)
    summed = jnp.einsum(
        "ctq,cqrw->ctrw", assign, received, preferred_element_type=jnp.float32
    ).astype(jnp.bfloat16)
    returned = lax.all_to_all(summed, "sector", split_axis=1, concat_axis=1, tiled=True)
    gathered_cols = returned.reshape(channels, bond_dim, col_width)
    arrived = lax.all_to_all(gathered_cols, "shard", split_axis=1, concat_axis=2, tiled=True)
    local_rows = arrived.shape[1]
    phys_count = arrived.shape[2] // bond_dim
    stacked = arrived.reshape(channels, local_rows, phys_count, bond_dim)
    env_rows = lax.all_gather(right_environment[:, 0], "shard", axis=1, tiled=True)
    row_ids = jnp.arange(env_rows.shape[1], dtype=jnp.int32)
    keep_mask = (row_ids < right_live[group_index])[None, :, None] & own_right[None, None, :]
    env_live = jnp.where(keep_mask, env_rows, jnp.zeros_like(env_rows))
    result = jnp.einsum("crpk,cnk->rpn", stacked, env_live, preferred_element_type=jnp.float32)
    return result.reshape(1, local_rows, phys_count * bond_dim).astype(jnp.bfloat16)


def fits(mesh, shape):
    blocks, shards_n = mesh.shape["sector"], mesh.shape["shard"]
    bond = shape[1]
    local = shape[2] // shards_n
    if local % bond or bond % shards_n or not (is_pow2(blocks) and is_pow2(shards_n)) or shards_n != 8:
        return False
    col_parts = local // bond
    return blocks % col_parts == 0 and is_pow2(col_parts) and (bond // shards_n) % (blocks // col_parts * 16) == 0


def solution(mesh):
    def whole(*arrays):
        quick = fits(mesh, arrays[0].shape)
        mapped = jax.shard_map(
            fast if quick else shards,
            mesh=mesh,
            in_specs=(
                P("sector", None, "shard"),
                P(None, "sector", "shard", None),
                P(None, "sector", "shard", None),
                P(),
                P(),
            ),
            out_specs=P("sector", "shard", None),
            check_vma=False,
        )
        return mapped(*arrays)

    return whole
```

time: 215 us -> 208 us (0.967)
  waiting for transfers between devices: 102 us -> 94 us
  local copies, waits for them, and re-layouts: 9.5 us -> 4.43 us
  starting transfers between devices: 75.7 us -> 79.1 us
    ppermute x71 -> x70, waiting for transfers between devices: 102 us -> 94 us  [exchange(): return lax.ppermute(x, axis, [(a, a ^ offset) for a in range(size)])]
    ppermute x71 -> x70, starting transfers between devices: 75.7 us -> 79.1 us  [exchange(): return lax.ppermute(x, axis, [(a, a ^ offset) for a in range(size)])]
    pallas_call x4 -> x5, Pallas kernels: 10.8 us -> 12.3 us  [the longest x2 6.37 us: destination_sums(): pl.pallas_call(functools.partial(sum_kernel, blocks=blocks, own_n=own_n,...]
  transfers between devices with their start and end apart: 71 -> 70, of which waited for: 19 -> 26; matrix products, arithmetic and copies ran while one was open for 1% -> 0% of each run, Pallas kernels for 10% -> 12%
where the time goes in v1:
time: 208 us; the launch traced here: 206 us
  waiting for transfers between devices  94 us (45%)
  starting transfers between devices  79.1 us (38%)
  Pallas kernels  27.2 us (13%)
  local copies, waits for them, and re-layouts  4.43 us (2%)
    ppermute x70, waiting for transfers between devices, exchange(): return lax.ppermute(x, axis, [(a, a ^ offset) for a in range(size)])  94 us
    ppermute x70, starting transfers between devices, exchange(): return lax.ppermute(x, axis, [(a, a ^ offset) for a in range(size)])  79.1 us
    pallas_call x2, Pallas kernels, products(): pl.pallas_call(functools.partial(products_kernel, shards_n=shards_n, row_...  14.9 us
    pallas_call x2, Pallas kernels, destination_sums(): pl.pallas_call(functools.partial(sum_kernel, blocks=blocks, own_n=own_n,...  6.37 us
  transfers between devices with their start and end apart: 70, of which 26 were waited for; matrix products, arithmetic and copies ran while one was open for 0% of the time, Pallas kernels for 12%

profile of v1, /device:TPU:0, one launch (start us, length us, event | category | flops | bytes accessed | tf_op | source)
XLA Modules:
  0.0 205.6 jit_solution(11510004652324225430)
XLA Ops:
  1.8 3.0 %collective-permute-start.7 = (bf16[96,768]{1,0:T(8,128)(2,1)}, bf16[96,768]{1,0:T(8,128)(2,1)S(1)}, u32[]{:S(2)}, u32[]{:S(2)}) collective-permute-start(bf16[96,768]{1,0:T(8,128)(2,1)} %get-tuple-element.35.refs_0_), channel_id=1, source_target_pairs={{0,8},{8,0},{16,24},{24,16},{1,9},{9,1},{17,25},{25,17},{2,10},{10... | collective-permute-start | bytes 442376 | tf_op jit(solution)/shard_map/ppermute | solution.py:17
  8.4 2.6 %collective-permute-start.3 = (bf16[96,768]{1,0:T(8,128)(2,1)}, bf16[96,768]{1,0:T(8,128)(2,1)S(1)}, u32[]{:S(2)}, u32[]{:S(2)}) collective-permute-start(bf16[96,768]{1,0:T(8,128)(2,1)} %get-tuple-element.34.refs_0_), channel_id=1, source_target_pairs={{0,4},{1,5},{2,6},{3,7},{4,0},{5,1},{6,2},{7,3},{8,12},{9,13},{10,... | collective-permute-start | bytes 442376 | tf_op jit(solution)/shard_map/ppermute | solution.py:17
  17.0 4.9 %collective-permute-done.3.refs_4_ = bf16[96,768]{1,0:T(8,128)(2,1)S(1)} collective-permute-done((bf16[96,768]{1,0:T(8,128)(2,1)}, bf16[96,768]{1,0:T(8,128)(2,1)S(1)}, u32[]{:S(2)}, u32[]{:S(2)}) %collective-permute-start.3) | collective-permute-done | bytes 147488 | tf_op jit(solution)/shard_map/ppermute | solution.py:17
  24.1 2.9 %collective-permute-start.13 = (bf16[96,768]{1,0:T(8,128)(2,1)}, bf16[96,768]{1,0:T(8,128)(2,1)S(1)}, u32[]{:S(2)}, u32[]{:S(2)}) collective-permute-start(bf16[96,768]{1,0:T(8,128)(2,1)} %mask_right.2.refs_8_), channel_id=1, source_target_pairs={{0,4},{1,5},{2,6},{3,7},{4,0},{5,1},{6,2},{7,3},{8,12},{9,13},{10,... | collective-permute-start | bytes 442376 | tf_op jit(solution)/shard_map/ppermute | solution.py:17
  33.1 5.2 %collective-permute-done.13.refs_12_ = bf16[96,768]{1,0:T(8,128)(2,1)S(1)} collective-permute-done((bf16[96,768]{1,0:T(8,128)(2,1)}, bf16[96,768]{1,0:T(8,128)(2,1)S(1)}, u32[]{:S(2)}, u32[]{:S(2)}) %collective-permute-start.13) | collective-permute-done | bytes 147488 | tf_op jit(solution)/shard_map/ppermute | solution.py:17
  39.7 3.4 %collective-permute-start.26 = (bf16[2,96,768]{2,1,0:T(8,128)(2,1)}, bf16[2,96,768]{2,1,0:T(8,128)(2,1)S(1)}, u32[]{:S(2)}, u32[]{:S(2)}) collective-permute-start(bf16[2,96,768]{2,1,0:T(8,128)(2,1)} %mask_right.3.refs_0_), channel_id=1, source_target_pairs={{0,4},{1,5},{2,6},{3,7},{4,0},{5,1},{6,2},{7,3},{8,12},{9,13},{10,... | collective-permute-start | bytes 884744 | tf_op jit(solution)/shard_map/ppermute | solution.py:17
  47.6 7.6 %products.2 = (bf16[384,768]{1,0:T(8,128)(2,1)}, bf16[384,768]{1,0:T(8,128)(2,1)}, bf16[384,768]{1,0:T(8,128)(2,1)}, bf16[384,768]{1,0:T(8,128)(2,1)}) custom-call(bf16[96,768]{1,0:T(8,128)(2,1)} %get-tuple-element.34.refs_0_, bf16[96,768]{1,0:T(8,128)(2,1)} %copy-done.20, bf16[96,768]{1,0:T(8,128)(2,1)} %copy-done.17, bf16[96,768]{1,0:T(8,128)(2,1)} %copy-done.25, ...), custom_call_target="tpu_custom_call" | custom-call | tf_op jit(solution)/shard_map/products/pallas_call | solution.py:131
  56.7 7.1 %collective-permute-done.26.refs_4_ = bf16[2,96,768]{2,1,0:T(8,128)(2,1)S(1)} collective-permute-done((bf16[2,96,768]{2,1,0:T(8,128)(2,1)}, bf16[2,96,768]{2,1,0:T(8,128)(2,1)S(1)}, u32[]{:S(2)}, u32[]{:S(2)}) %collective-permute-start.26) | collective-permute-done | bytes 294944 | tf_op jit(solution)/shard_map/ppermute | solution.py:17
  69.9 7.3 %products.3 = (bf16[192,768]{1,0:T(8,128)(2,1)}, bf16[192,768]{1,0:T(8,128)(2,1)}, bf16[192,768]{1,0:T(8,128)(2,1)}, bf16[192,768]{1,0:T(8,128)(2,1)}, bf16[192,...) custom-call(bf16[2,96,768]{2,1,0:T(8,128)(2,1)} %mask_right.3.refs_0_, ...), custom_call_target="tpu_custom_call" | custom-call | tf_op jit(solution)/shard_map/products/pallas_call | solution.py:131
  80.7 18.5 %collective-permute-done.18.refs_2_ = bf16[384,768]{1,0:T(8,128)(2,1)S(1)} collective-permute-done((bf16[384,768]{1,0:T(8,128)(2,1)}, bf16[384,768]{1,0:T(8,128)(2,1)S(1)}, u32[]{:S(2)}, u32[]{:S(2)}) %collective-permute-start.18) | collective-permute-done | bytes 589856 | tf_op jit(solution)/shard_map/ppermute | solution.py:17
  102.7 8.3 %collective-permute-done.31.refs_6_ = bf16[192,768]{1,0:T(8,128)(2,1)S(1)} collective-permute-done((bf16[192,768]{1,0:T(8,128)(2,1)}, bf16[192,768]{1,0:T(8,128)(2,1)S(1)}, u32[]{:S(2)}, u32[]{:S(2)}) %collective-permute-start.31) | collective-permute-done | bytes 294944 | tf_op jit(solution)/shard_map/ppermute | solution.py:17
  111.8 3.3 %destination_sums.2 = (bf16[192,768]{1,0:T(8,128)(2,1)}, bf16[192,768]{1,0:T(8,128)(2,1)}, bf16[192,768]{1,0:T(8,128)(2,1)}, bf16[48,768]{1,0:T(8,128)(2,1)}, bf...) custom-call(s32[2,4]{1,0:T(2,128)} %targets.9, ...), custom_call_target="tpu_custom_call" | custom-call | tf_op jit(solution)/shard_map/destination_sums/pallas_call | solution.py:166
  115.4 3.2 %collective-permute-start.35 = (bf16[48,768]{1,0:T(8,128)(2,1)}, bf16[48,768]{1,0:T(8,128)(2,1)S(1)}, u32[]{:S(2)}, u32[]{:S(2)}) collective-permute-start(bf16[48,768]{1,0:T(8,128)(2,1)} %get-tuple-element.47), channel_id=1, source_target_pairs={{0,4},{1,5},{2,6},{3,7},{4,0},{5,1},{6,2},{7,3},{8,12},{9,13},{10,... | collective-permute-start | bytes 221192 | tf_op jit(solution)/shard_map/ppermute | solution.py:17
  121.1 3.1 %destination_sums.3 = (bf16[192,768]{1,0:T(8,128)(2,1)}, bf16[192,768]{1,0:T(8,128)(2,1)}, bf16[192,768]{1,0:T(8,128)(2,1)}, bf16[48,768]{1,0:T(8,128)(2,1)}, bf...) custom-call(s32[2,4]{1,0:T(2,128)} %targets.9, ...), custom_call_target="tpu_custom_call" | custom-call | tf_op jit(solution)/shard_map/destination_sums/pallas_call | solution.py:166
  127.3 2.6 %collective-permute-start.56 = (bf16[48,768]{1,0:T(8,128)(2,1)S(1)}, bf16[48,768]{1,0:T(8,128)(2,1)S(1)}, u32[]{:S(2)}, u32[]{:S(2)}) collective-permute-start(bf16[48,768]{1,0:T(8,128)(2,1)S(1)} %copy-done.44), channel_id=1, source_target_pairs={{0,6},{1,7},{2,4},{3,5},{4,2},{5,3},{6,0},{7,1},{8,14},{9,15},{10,... | collective-permute-start | bytes 221192 | tf_op jit(solution)/shard_map/ppermute | solution.py:17
  131.3 7.5 %collective-permute-done.42 = bf16[192,768]{1,0:T(8,128)(2,1)S(1)} collective-permute-done((bf16[192,768]{1,0:T(8,128)(2,1)S(1)}, bf16[192,768]{1,0:T(8,128)(2,1)S(1)}, u32[]{:S(2)}, u32[]{:S(2)}) %collective-permute-start.42) | collective-permute-done | bytes 294944 | tf_op jit(solution)/shard_map/ppermute | solution.py:17
  141.0 5.4 %collective-permute-done.62 = bf16[192,768]{1,0:T(8,128)(2,1)S(1)} collective-permute-done((bf16[192,768]{1,0:T(8,128)(2,1)S(1)}, bf16[192,768]{1,0:T(8,128)(2,1)S(1)}, u32[]{:S(2)}, u32[]{:S(2)}) %collective-permute-start.62) | collective-permute-done | bytes 294944 | tf_op jit(solution)/shard_map/ppermute | solution.py:17
  148.5 3.0 %collective-permute-start.38 = (bf16[48,768]{1,0:T(8,128)(2,1)S(1)}, bf16[48,768]{1,0:T(8,128)(2,1)S(1)}, u32[]{:S(2)}, u32[]{:S(2)}) collective-permute-start(bf16[48,768]{1,0:T(8,128)(2,1)S(1)} %get-tuple-element.83), channel_id=1, source_target_pairs={{0,2},{1,3},{2,0},{3,1},{4,6},{5,7},{6,4},{7,5},{8,10},{9,11},{10,... | collective-permute-start | bytes 221192 | tf_op jit(solution)/shard_map/ppermute | solution.py:17
  154.7 3.4 %collective-permute-start.40 = (bf16[48,768]{1,0:T(8,128)(2,1)S(1)}, bf16[48,768]{1,0:T(8,128)(2,1)S(1)}, u32[]{:S(2)}, u32[]{:S(2)}) collective-permute-start(bf16[48,768]{1,0:T(8,128)(2,1)S(1)} %get-tuple-element.81), channel_id=1, source_target_pairs={{0,4},{1,5},{2,6},{3,7},{4,0},{5,1},{6,2},{7,3},{8,12},{9,13},{10,... | collective-permute-start | bytes 221192 | tf_op jit(solution)/shard_map/ppermute | solution.py:17
  160.5 3.0 %collective-permute-start.43 = (bf16[48,768]{1,0:T(8,128)(2,1)S(1)}, bf16[48,768]{1,0:T(8,128)(2,1)S(1)}, u32[]{:S(2)}, u32[]{:S(2)}) collective-permute-start(bf16[48,768]{1,0:T(8,128)(2,1)S(1)} %get-tuple-element.79), channel_id=1, source_target_pairs={{0,2},{1,3},{2,0},{3,1},{4,6},{5,7},{6,4},{7,5},{8,10},{9,11},{10,... | collective-permute-start | bytes 221192 | tf_op jit(solution)/shard_map/ppermute | solution.py:17
  163.5 3.0 %collective-permute-done.41 = bf16[48,768]{1,0:T(8,128)(2,1)S(1)} collective-permute-done((bf16[48,768]{1,0:T(8,128)(2,1)S(1)}, bf16[48,768]{1,0:T(8,128)(2,1)S(1)}, u32[]{:S(2)}, u32[]{:S(2)}) %collective-permute-start.41) | collective-permute-done | bytes 73760 | tf_op jit(solution)/shard_map/ppermute | solution.py:17
  170.9 5.4 %collective-permute-done.45 = bf16[48,768]{1,0:T(8,128)(2,1)S(1)} collective-permute-done((bf16[48,768]{1,0:T(8,128)(2,1)S(1)}, bf16[48,768]{1,0:T(8,128)(2,1)S(1)}, u32[]{:S(2)}, u32[]{:S(2)}) %collective-permute-start.45) | collective-permute-done | bytes 73760 | tf_op jit(solution)/shard_map/ppermute | solution.py:17
  177.3 3.7 %collective-permute-done.48 = bf16[48,768]{1,0:T(8,128)(2,1)S(1)} collective-permute-done((bf16[48,768]{1,0:T(8,128)(2,1)S(1)}, bf16[48,768]{1,0:T(8,128)(2,1)S(1)}, u32[]{:S(2)}, u32[]{:S(2)}) %collective-permute-start.48) | collective-permute-done | bytes 73760 | tf_op jit(solution)/shard_map/ppermute | solution.py:17
  181.9 6.7 %collective-permute-done.50 = bf16[48,768]{1,0:T(8,128)(2,1)S(1)} collective-permute-done((bf16[48,768]{1,0:T(8,128)(2,1)S(1)}, bf16[48,768]{1,0:T(8,128)(2,1)S(1)}, u32[]{:S(2)}, u32[]{:S(2)}) %collective-permute-start.50) | collective-permute-done | bytes 73760 | tf_op jit(solution)/shard_map/ppermute | solution.py:17
  (254 shorter events, 80.5 us)
Async XLA Ops:
  8.4 13.5 %collective-permute-start.3 = (bf16[96,768]{1,0:T(8,128)(2,1)}, bf16[96,768]{1,0:T(8,128)(2,1)S(1)}, u32[]{:S(2)}, u32[]{:S(2)}) collective-permute-start(bf16[96,768]{1,0:T(8,128)(2,1)} %get-tuple-element.34.refs_0_), channel_id=1, source_target_pairs={{0,4},{1,5},{2,6},{3,7},{4,0},{5,1},{6,2},{7,3},{8,12},{9,13},{10,... | collective-permute-start | bytes 442376 | tf_op jit(solution)/shard_map/ppermute | solution.py:17
  11.0 12.9 %collective-permute-start.5 = (bf16[96,768]{1,0:T(8,128)(2,1)}, bf16[96,768]{1,0:T(8,128)(2,1)S(1)}, u32[]{:S(2)}, u32[]{:S(2)}) collective-permute-start(bf16[96,768]{1,0:T(8,128)(2,1)} %get-tuple-element.34.refs_0_), channel_id=1, source_target_pairs={{0,6},{1,7},{2,4},{3,5},{4,2},{5,3},{6,0},{7,1},{8,14},{9,15},{10,... | collective-permute-start | bytes 442376 | tf_op jit(solution)/shard_map/ppermute | solution.py:17
  15.3 11.6 %collective-permute-start.21 = (bf16[96,768]{1,0:T(8,128)(2,1)}, bf16[96,768]{1,0:T(8,128)(2,1)S(1)}, u32[]{:S(2)}, u32[]{:S(2)}) collective-permute-start(bf16[96,768]{1,0:T(8,128)(2,1)} %get-tuple-element.40.refs_0_), channel_id=1, source_target_pairs={{0,16},{8,24},{16,0},{24,8},{1,17},{9,25},{17,1},{25,9},{2,18},{10... | collective-permute-start | bytes 442376 | tf_op jit(solution)/shard_map/ppermute | solution.py:17
  24.1 14.2 %collective-permute-start.13 = (bf16[96,768]{1,0:T(8,128)(2,1)}, bf16[96,768]{1,0:T(8,128)(2,1)S(1)}, u32[]{:S(2)}, u32[]{:S(2)}) collective-permute-start(bf16[96,768]{1,0:T(8,128)(2,1)} %mask_right.2.refs_8_), channel_id=1, source_target_pairs={{0,4},{1,5},{2,6},{3,7},{4,0},{5,1},{6,2},{7,3},{8,12},{9,13},{10,... | collective-permute-start | bytes 442376 | tf_op jit(solution)/shard_map/ppermute | solution.py:17
  31.2 13.4 %collective-permute-start.24 = (bf16[2,96,768]{2,1,0:T(8,128)(2,1)}, bf16[2,96,768]{2,1,0:T(8,128)(2,1)S(1)}, u32[]{:S(2)}, u32[]{:S(2)}) collective-permute-start(bf16[2,96,768]{2,1,0:T(8,128)(2,1)} %mask_right.3.refs_0_), channel_id=1, source_target_pairs={{0,2},{1,3},{2,0},{3,1},{4,6},{5,7},{6,4},{7,5},{8,10},{9,11},{10,... | collective-permute-start | bytes 884744 | tf_op jit(solution)/shard_map/ppermute | solution.py:17
  39.7 24.1 %collective-permute-start.26 = (bf16[2,96,768]{2,1,0:T(8,128)(2,1)}, bf16[2,96,768]{2,1,0:T(8,128)(2,1)S(1)}, u32[]{:S(2)}, u32[]{:S(2)}) collective-permute-start(bf16[2,96,768]{2,1,0:T(8,128)(2,1)} %mask_right.3.refs_0_), channel_id=1, source_target_pairs={{0,4},{1,5},{2,6},{3,7},{4,0},{5,1},{6,2},{7,3},{8,12},{9,13},{10,... | collective-permute-start | bytes 884744 | tf_op jit(solution)/shard_map/ppermute | solution.py:17
  43.1 22.2 %collective-permute-start.28 = (bf16[2,96,768]{2,1,0:T(8,128)(2,1)}, bf16[2,96,768]{2,1,0:T(8,128)(2,1)S(1)}, u32[]{:S(2)}, u32[]{:S(2)}) collective-permute-start(bf16[2,96,768]{2,1,0:T(8,128)(2,1)} %mask_right.3.refs_0_), channel_id=1, source_target_pairs={{0,6},{1,7},{2,4},{3,5},{4,2},{5,3},{6,0},{7,1},{8,14},{9,15},{10,... | collective-permute-start | bytes 884744 | tf_op jit(solution)/shard_map/ppermute | solution.py:17
  44.5 22.3 %collective-permute-start.23 = (bf16[2,96,768]{2,1,0:T(8,128)(2,1)}, bf16[2,96,768]{2,1,0:T(8,128)(2,1)S(1)}, u32[]{:S(2)}, u32[]{:S(2)}) collective-permute-start(bf16[2,96,768]{2,1,0:T(8,128)(2,1)} %mask_right.3.refs_0_), channel_id=1, source_target_pairs={{0,1},{1,0},{2,3},{3,2},{4,5},{5,4},{6,7},{7,6},{8,9},{9,8},{10,11... | collective-permute-start | bytes 884744 | tf_op jit(solution)/shard_map/ppermute | solution.py:17
  44.5 22.2 %collective-permute-start.25 = (bf16[2,96,768]{2,1,0:T(8,128)(2,1)S(1)}, bf16[2,96,768]{2,1,0:T(8,128)(2,1)S(1)}, u32[]{:S(2)}, u32[]{:S(2)}) collective-permute-start(bf16[2,96,768]{2,1,0:T(8,128)(2,1)S(1)} %collective-permute-done.24.refs_2_), channel_id=1, source_target_pairs={{0,1},{1,0},{2,3},{3,2},{4,5},{5,4},{6,7},{7,6},{8,9},{9,8},{10,11... | collective-permute-start | bytes 884744 | tf_op jit(solution)/shard_map/ppermute | solution.py:17
  55.2 24.0 %collective-permute-start.17 = (bf16[384,768]{1,0:T(8,128)(2,1)}, bf16[384,768]{1,0:T(8,128)(2,1)S(1)}, u32[]{:S(2)}, u32[]{:S(2)}) collective-permute-start(bf16[384,768]{1,0:T(8,128)(2,1)} %get-tuple-element.37), channel_id=1, source_target_pairs={{0,8},{8,0},{16,24},{24,16},{1,9},{9,1},{17,25},{25,17},{2,10},{10... | collective-permute-start | bytes 1769480 | tf_op jit(solution)/shard_map/ppermute | solution.py:17
  63.8 35.4 %collective-permute-start.18 = (bf16[384,768]{1,0:T(8,128)(2,1)}, bf16[384,768]{1,0:T(8,128)(2,1)S(1)}, u32[]{:S(2)}, u32[]{:S(2)}) collective-permute-start(bf16[384,768]{1,0:T(8,128)(2,1)} %get-tuple-element.38), channel_id=1, source_target_pairs={{0,16},{8,24},{16,0},{24,8},{1,17},{9,25},{17,1},{25,9},{2,18},{10... | collective-permute-start | bytes 1769480 | tf_op jit(solution)/shard_map/ppermute | solution.py:17
  65.3 35.3 %collective-permute-start.19 = (bf16[384,768]{1,0:T(8,128)(2,1)}, bf16[384,768]{1,0:T(8,128)(2,1)S(1)}, u32[]{:S(2)}, u32[]{:S(2)}) collective-permute-start(bf16[384,768]{1,0:T(8,128)(2,1)} %get-tuple-element.39), channel_id=1, source_target_pairs={{0,24},{8,16},{16,8},{24,0},{1,25},{9,17},{17,9},{25,1},{2,26},{10... | collective-permute-start | bytes 1769480 | tf_op jit(solution)/shard_map/ppermute | solution.py:17
  77.2 25.0 %collective-permute-start.30 = (bf16[192,768]{1,0:T(8,128)(2,1)}, bf16[192,768]{1,0:T(8,128)(2,1)S(1)}, u32[]{:S(2)}, u32[]{:S(2)}) collective-permute-start(bf16[192,768]{1,0:T(8,128)(2,1)} %get-tuple-element.42), channel_id=1, source_target_pairs={{0,8},{8,0},{16,24},{24,16},{1,9},{9,1},{17,25},{25,17},{2,10},{10... | collective-permute-start | bytes 884744 | tf_op jit(solution)/shard_map/ppermute | solution.py:17
  77.7 33.3 %collective-permute-start.31 = (bf16[192,768]{1,0:T(8,128)(2,1)}, bf16[192,768]{1,0:T(8,128)(2,1)S(1)}, u32[]{:S(2)}, u32[]{:S(2)}) collective-permute-start(bf16[192,768]{1,0:T(8,128)(2,1)} %get-tuple-element.43), channel_id=1, source_target_pairs={{0,16},{8,24},{16,0},{24,8},{1,17},{9,25},{17,1},{25,9},{2,18},{10... | collective-permute-start | bytes 884744 | tf_op jit(solution)/shard_map/ppermute | solution.py:17
  79.2 31.7 %collective-permute-start.32 = (bf16[192,768]{1,0:T(8,128)(2,1)}, bf16[192,768]{1,0:T(8,128)(2,1)S(1)}, u32[]{:S(2)}, u32[]{:S(2)}) collective-permute-start(bf16[192,768]{1,0:T(8,128)(2,1)} %get-tuple-element.44), channel_id=1, source_target_pairs={{0,24},{8,16},{16,8},{24,0},{1,25},{9,17},{17,9},{25,1},{2,26},{10... | collective-permute-start | bytes 884744 | tf_op jit(solution)/shard_map/ppermute | solution.py:17
  99.2 16.2 %collective-permute-start.52 = (bf16[192,768]{1,0:T(8,128)(2,1)}, bf16[192,768]{1,0:T(8,128)(2,1)S(1)}, u32[]{:S(2)}, u32[]{:S(2)}) collective-permute-start(bf16[192,768]{1,0:T(8,128)(2,1)} %get-tuple-element.53), channel_id=1, source_target_pairs={{0,8},{8,0},{16,24},{24,16},{1,9},{9,1},{17,25},{25,17},{2,10},{10... | collective-permute-start | bytes 884744 | tf_op jit(solution)/shard_map/ppermute | solution.py:17
  100.7 18.0 %collective-permute-start.53 = (bf16[192,768]{1,0:T(8,128)(2,1)}, bf16[192,768]{1,0:T(8,128)(2,1)S(1)}, u32[]{:S(2)}, u32[]{:S(2)}) collective-permute-start(bf16[192,768]{1,0:T(8,128)(2,1)} %get-tuple-element.54), channel_id=1, source_target_pairs={{0,16},{8,24},{16,0},{24,8},{1,17},{9,25},{17,1},{25,9},{2,18},{10... | collective-permute-start | bytes 884744 | tf_op jit(solution)/shard_map/ppermute | solution.py:17
  102.2 17.3 %collective-permute-start.54 = (bf16[192,768]{1,0:T(8,128)(2,1)}, bf16[192,768]{1,0:T(8,128)(2,1)S(1)}, u32[]{:S(2)}, u32[]{:S(2)}) collective-permute-start(bf16[192,768]{1,0:T(8,128)(2,1)} %get-tuple-element.55), channel_id=1, source_target_pairs={{0,24},{8,16},{16,8},{24,0},{1,25},{9,17},{17,9},{25,1},{2,26},{10... | collective-permute-start | bytes 884744 | tf_op jit(solution)/shard_map/ppermute | solution.py:17
  115.4 11.8 %collective-permute-start.35 = (bf16[48,768]{1,0:T(8,128)(2,1)}, bf16[48,768]{1,0:T(8,128)(2,1)S(1)}, u32[]{:S(2)}, u32[]{:S(2)}) collective-permute-start(bf16[48,768]{1,0:T(8,128)(2,1)} %get-tuple-element.47), channel_id=1, source_target_pairs={{0,4},{1,5},{2,6},{3,7},{4,0},{5,1},{6,2},{7,3},{8,12},{9,13},{10,... | collective-permute-start | bytes 221192 | tf_op jit(solution)/shard_map/ppermute | solution.py:17
  124.2 14.6 %collective-permute-start.42 = (bf16[192,768]{1,0:T(8,128)(2,1)S(1)}, bf16[192,768]{1,0:T(8,128)(2,1)S(1)}, u32[]{:S(2)}, u32[]{:S(2)}) collective-permute-start(bf16[192,768]{1,0:T(8,128)(2,1)S(1)} %copy-done.39), channel_id=1, source_target_pairs={{0,16},{8,24},{16,0},{24,8},{1,17},{9,25},{17,1},{25,9},{2,18},{10... | collective-permute-start | bytes 884744 | tf_op jit(solution)/shard_map/ppermute | solution.py:17
  126.9 21.5 %collective-permute-start.47 = (bf16[192,768]{1,0:T(8,128)(2,1)S(1)}, bf16[192,768]{1,0:T(8,128)(2,1)S(1)}, u32[]{:S(2)}, u32[]{:S(2)}) collective-permute-start(bf16[192,768]{1,0:T(8,128)(2,1)S(1)} %copy-done.38), channel_id=1, source_target_pairs={{0,24},{8,16},{16,8},{24,0},{1,25},{9,17},{17,9},{25,1},{2,26},{10... | collective-permute-start | bytes 884744 | tf_op jit(solution)/shard_map/ppermute | solution.py:17
  127.2 63.2 %collective-permute-start.55 = (bf16[48,768]{1,0:T(8,128)(2,1)S(1)}, bf16[48,768]{1,0:T(8,128)(2,1)S(1)}, u32[]{:S(2)}, u32[]{:S(2)}) collective-permute-start(bf16[48,768]{1,0:T(8,128)(2,1)S(1)} %copy-done.45), channel_id=1, source_target_pairs={{0,1},{1,0},{2,3},{3,2},{4,5},{5,4},{6,7},{7,6},{8,9},{9,8},{10,11... | collective-permute-start | bytes 221192 | tf_op jit(solution)/shard_map/ppermute | solution.py:17
  127.3 65.3 %collective-permute-start.56 = (bf16[48,768]{1,0:T(8,128)(2,1)S(1)}, bf16[48,768]{1,0:T(8,128)(2,1)S(1)}, u32[]{:S(2)}, u32[]{:S(2)}) collective-permute-start(bf16[48,768]{1,0:T(8,128)(2,1)S(1)} %copy-done.44), channel_id=1, source_target_pairs={{0,6},{1,7},{2,4},{3,5},{4,2},{5,3},{6,0},{7,1},{8,14},{9,15},{10,... | collective-permute-start | bytes 221192 | tf_op jit(solution)/shard_map/ppermute | solution.py:17
  140.7 52.3 %collective-permute-start.57 = (bf16[48,768]{1,0:T(8,128)(2,1)S(1)}, bf16[48,768]{1,0:T(8,128)(2,1)S(1)}, u32[]{:S(2)}, u32[]{:S(2)}) collective-permute-start(bf16[48,768]{1,0:T(8,128)(2,1)S(1)} %copy-done.43), channel_id=1, source_target_pairs={{0,7},{1,6},{2,5},{3,4},{4,3},{5,2},{6,1},{7,0},{8,15},{9,14},{10,... | collective-permute-start | bytes 221192 | tf_op jit(solution)/shard_map/ppermute | solution.py:17
  (92 other events, 757.6 us)

commit v2 on v1

--- a/solution.py
+++ b/solution.py
@@ -89,8 +89,8 @@
 
 
 def shard_chunks(shards_n):
-    first = list(range(2, 2 + shards_n // 2))
-    return first, [m for m in range(shards_n) if m not in first]
+    first = [shards_n // 2, shards_n // 2 + 1, 2, 3]
+    return first, [m for m in reversed(range(shards_n)) if m not in first]
 
 
 def products_kernel(*refs, shards_n, row_parts, col_parts, parts):
@@ -213,7 +213,7 @@
         parts = [parts for channel in received for parts in channel]
         totals = destination_sums(
             targets, [p[u % len(p)] for p in parts], [0 if len(p) > 1 else u * chunk_rows for p in parts],
-            blocks, chunk_rows, len(chunk), 2)
+            blocks, chunk_rows, len(chunk), 1 + len(chunk) % 2 * (len(chunk) - 1) if len(chunk) % 2 else 2)
         for j in range(blocks):
             row_at = (own_row ^ (j // col_parts)) * sub
             col_at = (own_col ^ (j % col_parts)) * bond
@@ -280,7 +280,7 @@
     blocks, shards_n = mesh.shape["sector"], mesh.shape["shard"]
     bond = shape[1]
     local = shape[2] // shards_n
-    if local % bond or bond % shards_n or not (is_pow2(blocks) and is_pow2(shards_n)) or shards_n != 8:
+    if local % bond or bond % shards_n or not (is_pow2(blocks) and is_pow2(shards_n)) or shards_n != 8 or blocks != 4:
         return False
     col_parts = local // bond
     return blocks % col_parts == 0 and is_pow2(col_parts) and (bond // shards_n) % (blocks // col_parts * 16) == 0

time: 208 us -> 213 us (1.024)
  waiting for transfers between devices: 94 us -> 113 us
  starting transfers between devices: 79.1 us -> 63 us
  local copies, waits for them, and re-layouts: 4.43 us -> 6.63 us
    ppermute x70, waiting for transfers between devices: 94 us -> 113 us  [exchange(): return lax.ppermute(x, axis, [(a, a ^ offset) for a in range(size)])]
    ppermute x70, starting transfers between devices: 79.1 us -> 63 us  [exchange(): return lax.ppermute(x, axis, [(a, a ^ offset) for a in range(size)])]
    unnamed x92 -> x98, local copies, waits for them, and re-layouts: 3.18 us -> 5.37 us
  transfers between devices with their start and end apart: 70 -> 70, of which waited for: 26 -> 30; matrix products, arithmetic and copies ran while one was open for 0% -> 0% of each run, Pallas kernels for 12% -> 12%
where the time goes in v2:
time: 213 us; the launch traced here: 211 us
  waiting for transfers between devices  113 us (53%)
  starting transfers between devices  63 us (30%)
  Pallas kernels  27.2 us (13%)
  local copies, waits for them, and re-layouts  6.63 us (3%)
    ppermute x70, waiting for transfers between devices, exchange(): return lax.ppermute(x, axis, [(a, a ^ offset) for a in range(size)])  113 us
    ppermute x70, starting transfers between devices, exchange(): return lax.ppermute(x, axis, [(a, a ^ offset) for a in range(size)])  63 us
    pallas_call x2, Pallas kernels, products(): pl.pallas_call(functools.partial(products_kernel, shards_n=shards_n, row_...  14.9 us
    pallas_call x2, Pallas kernels, destination_sums(): pl.pallas_call(functools.partial(sum_kernel, blocks=blocks, own_n=own_n,...  6.39 us
    unnamed x98, local copies, waits for them, and re-layouts  5.37 us
  transfers between devices with their start and end apart: 70, of which 30 were waited for; matrix products, arithmetic and copies ran while one was open for 0% of the time, Pallas kernels for 12%

profile of v2, /device:TPU:0, one launch (start us, length us, event | category | flops | bytes accessed | tf_op | source)
XLA Modules:
  0.0 210.9 jit_solution(2034743098836162276)
XLA Ops:
  1.8 3.0 %collective-permute-start.7 = (bf16[96,768]{1,0:T(8,128)(2,1)}, bf16[96,768]{1,0:T(8,128)(2,1)S(1)}, u32[]{:S(2)}, u32[]{:S(2)}) collective-permute-start(bf16[96,768]{1,0:T(8,128)(2,1)} %get-tuple-element.35.refs_0_), channel_id=1, source_target_pairs={{0,8},{8,0},{16,24},{24,16},{1,9},{9,1},{17,25},{25,17},{2,10},{10... | collective-permute-start | bytes 442376 | tf_op jit(solution)/shard_map/ppermute | solution.py:17
  17.0 4.9 %collective-permute-done.3.refs_4_ = bf16[96,768]{1,0:T(8,128)(2,1)S(1)} collective-permute-done((bf16[96,768]{1,0:T(8,128)(2,1)}, bf16[96,768]{1,0:T(8,128)(2,1)S(1)}, u32[]{:S(2)}, u32[]{:S(2)}) %collective-permute-start.3) | collective-permute-done | bytes 147488 | tf_op jit(solution)/shard_map/ppermute | solution.py:17
  24.1 2.9 %collective-permute-start.13 = (bf16[96,768]{1,0:T(8,128)(2,1)}, bf16[96,768]{1,0:T(8,128)(2,1)S(1)}, u32[]{:S(2)}, u32[]{:S(2)}) collective-permute-start(bf16[96,768]{1,0:T(8,128)(2,1)} %mask_right.2.refs_8_), channel_id=1, source_target_pairs={{0,4},{1,5},{2,6},{3,7},{4,0},{5,1},{6,2},{7,3},{8,12},{9,13},{10,... | collective-permute-start | bytes 442376 | tf_op jit(solution)/shard_map/ppermute | solution.py:17
  33.1 5.2 %collective-permute-done.13.refs_12_ = bf16[96,768]{1,0:T(8,128)(2,1)S(1)} collective-permute-done((bf16[96,768]{1,0:T(8,128)(2,1)}, bf16[96,768]{1,0:T(8,128)(2,1)S(1)}, u32[]{:S(2)}, u32[]{:S(2)}) %collective-permute-start.13) | collective-permute-done | bytes 147488 | tf_op jit(solution)/shard_map/ppermute | solution.py:17
  39.7 3.4 %collective-permute-start.26 = (bf16[2,96,768]{2,1,0:T(8,128)(2,1)}, bf16[2,96,768]{2,1,0:T(8,128)(2,1)S(1)}, u32[]{:S(2)}, u32[]{:S(2)}) collective-permute-start(bf16[2,96,768]{2,1,0:T(8,128)(2,1)} %mask_right.3.refs_0_), channel_id=1, source_target_pairs={{0,4},{1,5},{2,6},{3,7},{4,0},{5,1},{6,2},{7,3},{8,12},{9,13},{10,... | collective-permute-start | bytes 884744 | tf_op jit(solution)/shard_map/ppermute | solution.py:17
  47.6 7.6 %products.2 = (bf16[384,768]{1,0:T(8,128)(2,1)}, bf16[384,768]{1,0:T(8,128)(2,1)}, bf16[384,768]{1,0:T(8,128)(2,1)}, bf16[384,768]{1,0:T(8,128)(2,1)}) custom-call(bf16[96,768]{1,0:T(8,128)(2,1)} %get-tuple-element.34.refs_0_, bf16[96,768]{1,0:T(8,128)(2,1)} %copy-done.20, bf16[96,768]{1,0:T(8,128)(2,1)} %copy-done.17, bf16[96,768]{1,0:T(8,128)(2,1)} %copy-done.25, ...), custom_call_target="tpu_custom_call" | custom-call | tf_op jit(solution)/shard_map/products/pallas_call | solution.py:131
  56.8 7.1 %collective-permute-done.26.refs_4_ = bf16[2,96,768]{2,1,0:T(8,128)(2,1)S(1)} collective-permute-done((bf16[2,96,768]{2,1,0:T(8,128)(2,1)}, bf16[2,96,768]{2,1,0:T(8,128)(2,1)S(1)}, u32[]{:S(2)}, u32[]{:S(2)}) %collective-permute-start.26) | collective-permute-done | bytes 294944 | tf_op jit(solution)/shard_map/ppermute | solution.py:17
  69.8 7.3 %products.3 = (bf16[192,768]{1,0:T(8,128)(2,1)}, bf16[192,768]{1,0:T(8,128)(2,1)}, bf16[192,768]{1,0:T(8,128)(2,1)}, bf16[192,768]{1,0:T(8,128)(2,1)}, bf16[192,...) custom-call(bf16[2,96,768]{2,1,0:T(8,128)(2,1)} %mask_right.3.refs_0_, ...), custom_call_target="tpu_custom_call" | custom-call | tf_op jit(solution)/shard_map/products/pallas_call | solution.py:131
  80.6 18.6 %collective-permute-done.18.refs_2_ = bf16[384,768]{1,0:T(8,128)(2,1)S(1)} collective-permute-done((bf16[384,768]{1,0:T(8,128)(2,1)}, bf16[384,768]{1,0:T(8,128)(2,1)S(1)}, u32[]{:S(2)}, u32[]{:S(2)}) %collective-permute-start.18) | collective-permute-done | bytes 589856 | tf_op jit(solution)/shard_map/ppermute | solution.py:17
  102.7 8.3 %collective-permute-done.31.refs_6_ = bf16[192,768]{1,0:T(8,128)(2,1)S(1)} collective-permute-done((bf16[192,768]{1,0:T(8,128)(2,1)}, bf16[192,768]{1,0:T(8,128)(2,1)S(1)}, u32[]{:S(2)}, u32[]{:S(2)}) %collective-permute-start.31) | collective-permute-done | bytes 294944 | tf_op jit(solution)/shard_map/ppermute | solution.py:17
  111.8 3.2 %destination_sums.2 = (bf16[192,768]{1,0:T(8,128)(2,1)}, bf16[192,768]{1,0:T(8,128)(2,1)}, bf16[192,768]{1,0:T(8,128)(2,1)}, bf16[48,768]{1,0:T(8,128)(2,1)}, bf...) custom-call(s32[2,4]{1,0:T(2,128)} %targets.9, ...), custom_call_target="tpu_custom_call" | custom-call | tf_op jit(solution)/shard_map/destination_sums/pallas_call | solution.py:166
  117.6 3.1 %destination_sums.3 = (bf16[192,768]{1,0:T(8,128)(2,1)}, bf16[192,768]{1,0:T(8,128)(2,1)}, bf16[192,768]{1,0:T(8,128)(2,1)}, bf16[48,768]{1,0:T(8,128)(2,1)}, bf...) custom-call(s32[2,4]{1,0:T(2,128)} %targets.9, ...), custom_call_target="tpu_custom_call" | custom-call | tf_op jit(solution)/shard_map/destination_sums/pallas_call | solution.py:166
  120.9 3.1 %collective-permute-start.34 = (bf16[48,768]{1,0:T(8,128)(2,1)S(1)}, bf16[48,768]{1,0:T(8,128)(2,1)S(1)}, u32[]{:S(2)}, u32[]{:S(2)}) collective-permute-start(bf16[48,768]{1,0:T(8,128)(2,1)S(1)} %copy-done.48), channel_id=1, source_target_pairs={{0,5},{1,4},{2,7},{3,6},{4,1},{5,0},{6,3},{7,2},{8,13},{9,12},{10,... | collective-permute-start | bytes 221192 | tf_op jit(solution)/shard_map/ppermute | solution.py:17
  126.8 3.7 %collective-permute-done.34 = bf16[48,768]{1,0:T(8,128)(2,1)S(1)} collective-permute-done((bf16[48,768]{1,0:T(8,128)(2,1)S(1)}, bf16[48,768]{1,0:T(8,128)(2,1)S(1)}, u32[]{:S(2)}, u32[]{:S(2)}) %collective-permute-start.34) | collective-permute-done | bytes 73760 | tf_op jit(solution)/shard_map/ppermute | solution.py:17
  136.5 9.7 %collective-permute-done.42 = bf16[192,768]{1,0:T(8,128)(2,1)S(1)} collective-permute-done((bf16[192,768]{1,0:T(8,128)(2,1)S(1)}, bf16[192,768]{1,0:T(8,128)(2,1)S(1)}, u32[]{:S(2)}, u32[]{:S(2)}) %collective-permute-start.42) | collective-permute-done | bytes 294944 | tf_op jit(solution)/shard_map/ppermute | solution.py:17
  148.1 6.5 %collective-permute-done.62 = bf16[192,768]{1,0:T(8,128)(2,1)S(1)} collective-permute-done((bf16[192,768]{1,0:T(8,128)(2,1)S(1)}, bf16[192,768]{1,0:T(8,128)(2,1)S(1)}, u32[]{:S(2)}, u32[]{:S(2)}) %collective-permute-start.62) | collective-permute-done | bytes 294944 | tf_op jit(solution)/shard_map/ppermute | solution.py:17
  157.1 5.9 %collective-permute-done.66 = bf16[192,768]{1,0:T(8,128)(2,1)S(1)} collective-permute-done((bf16[192,768]{1,0:T(8,128)(2,1)S(1)}, bf16[192,768]{1,0:T(8,128)(2,1)S(1)}, u32[]{:S(2)}, u32[]{:S(2)}) %collective-permute-start.66) | collective-permute-done | bytes 294944 | tf_op jit(solution)/shard_map/ppermute | solution.py:17
  163.1 4.9 %collective-permute-done.39 = bf16[48,768]{1,0:T(8,128)(2,1)S(1)} collective-permute-done((bf16[48,768]{1,0:T(8,128)(2,1)S(1)}, bf16[48,768]{1,0:T(8,128)(2,1)S(1)}, u32[]{:S(2)}, u32[]{:S(2)}) %collective-permute-start.39) | collective-permute-done | bytes 73760 | tf_op jit(solution)/shard_map/ppermute | solution.py:17
  168.7 4.4 %collective-permute-done.41 = bf16[48,768]{1,0:T(8,128)(2,1)S(1)} collective-permute-done((bf16[48,768]{1,0:T(8,128)(2,1)S(1)}, bf16[48,768]{1,0:T(8,128)(2,1)S(1)}, u32[]{:S(2)}, u32[]{:S(2)}) %collective-permute-start.41) | collective-permute-done | bytes 73760 | tf_op jit(solution)/shard_map/ppermute | solution.py:17
  173.1 3.2 %collective-permute-done.43 = bf16[48,768]{1,0:T(8,128)(2,1)S(1)} collective-permute-done((bf16[48,768]{1,0:T(8,128)(2,1)S(1)}, bf16[48,768]{1,0:T(8,128)(2,1)S(1)}, u32[]{:S(2)}, u32[]{:S(2)}) %collective-permute-start.43) | collective-permute-done | bytes 73760 | tf_op jit(solution)/shard_map/ppermute | solution.py:17
  180.6 3.1 %collective-permute-done.46 = bf16[48,768]{1,0:T(8,128)(2,1)S(1)} collective-permute-done((bf16[48,768]{1,0:T(8,128)(2,1)S(1)}, bf16[48,768]{1,0:T(8,128)(2,1)S(1)}, u32[]{:S(2)}, u32[]{:S(2)}) %collective-permute-start.46) | collective-permute-done | bytes 73760 | tf_op jit(solution)/shard_map/ppermute | solution.py:17
  186.2 3.7 %collective-permute-done.49 = bf16[48,768]{1,0:T(8,128)(2,1)S(1)} collective-permute-done((bf16[48,768]{1,0:T(8,128)(2,1)S(1)}, bf16[48,768]{1,0:T(8,128)(2,1)S(1)}, u32[]{:S(2)}, u32[]{:S(2)}) %collective-permute-start.49) | collective-permute-done | bytes 73760 | tf_op jit(solution)/shard_map/ppermute | solution.py:17
  190.8 3.4 %collective-permute-done.51 = bf16[48,768]{1,0:T(8,128)(2,1)S(1)} collective-permute-done((bf16[48,768]{1,0:T(8,128)(2,1)S(1)}, bf16[48,768]{1,0:T(8,128)(2,1)S(1)}, u32[]{:S(2)}, u32[]{:S(2)}) %collective-permute-start.51) | collective-permute-done | bytes 73760 | tf_op jit(solution)/shard_map/ppermute | solution.py:17
  195.3 3.0 %collective-permute-start.63 = (bf16[48,768]{1,0:T(8,128)(2,1)S(1)}, bf16[48,768]{1,0:T(8,128)(2,1)S(1)}, u32[]{:S(2)}, u32[]{:S(2)}) collective-permute-start(bf16[48,768]{1,0:T(8,128)(2,1)S(1)} %get-tuple-element.68), channel_id=1, source_target_pairs={{0,7},{1,6},{2,5},{3,4},{4,3},{5,2},{6,1},{7,0},{8,15},{9,14},{10,... | collective-permute-start | bytes 221192 | tf_op jit(solution)/shard_map/ppermute | solution.py:17
  (260 shorter events, 80.6 us)
Async XLA Ops:
  8.4 13.5 %collective-permute-start.3 = (bf16[96,768]{1,0:T(8,128)(2,1)}, bf16[96,768]{1,0:T(8,128)(2,1)S(1)}, u32[]{:S(2)}, u32[]{:S(2)}) collective-permute-start(bf16[96,768]{1,0:T(8,128)(2,1)} %get-tuple-element.34.refs_0_), channel_id=1, source_target_pairs={{0,4},{1,5},{2,6},{3,7},{4,0},{5,1},{6,2},{7,3},{8,12},{9,13},{10,... | collective-permute-start | bytes 442376 | tf_op jit(solution)/shard_map/ppermute | solution.py:17
  11.0 12.9 %collective-permute-start.5 = (bf16[96,768]{1,0:T(8,128)(2,1)}, bf16[96,768]{1,0:T(8,128)(2,1)S(1)}, u32[]{:S(2)}, u32[]{:S(2)}) collective-permute-start(bf16[96,768]{1,0:T(8,128)(2,1)} %get-tuple-element.34.refs_0_), channel_id=1, source_target_pairs={{0,6},{1,7},{2,4},{3,5},{4,2},{5,3},{6,0},{7,1},{8,14},{9,15},{10,... | collective-permute-start | bytes 442376 | tf_op jit(solution)/shard_map/ppermute | solution.py:17
  15.3 11.6 %collective-permute-start.21 = (bf16[96,768]{1,0:T(8,128)(2,1)}, bf16[96,768]{1,0:T(8,128)(2,1)S(1)}, u32[]{:S(2)}, u32[]{:S(2)}) collective-permute-start(bf16[96,768]{1,0:T(8,128)(2,1)} %get-tuple-element.40.refs_0_), channel_id=1, source_target_pairs={{0,16},{8,24},{16,0},{24,8},{1,17},{9,25},{17,1},{25,9},{2,18},{10... | collective-permute-start | bytes 442376 | tf_op jit(solution)/shard_map/ppermute | solution.py:17
  24.1 14.3 %collective-permute-start.13 = (bf16[96,768]{1,0:T(8,128)(2,1)}, bf16[96,768]{1,0:T(8,128)(2,1)S(1)}, u32[]{:S(2)}, u32[]{:S(2)}) collective-permute-start(bf16[96,768]{1,0:T(8,128)(2,1)} %mask_right.2.refs_8_), channel_id=1, source_target_pairs={{0,4},{1,5},{2,6},{3,7},{4,0},{5,1},{6,2},{7,3},{8,12},{9,13},{10,... | collective-permute-start | bytes 442376 | tf_op jit(solution)/shard_map/ppermute | solution.py:17
  31.2 13.3 %collective-permute-start.24 = (bf16[2,96,768]{2,1,0:T(8,128)(2,1)}, bf16[2,96,768]{2,1,0:T(8,128)(2,1)S(1)}, u32[]{:S(2)}, u32[]{:S(2)}) collective-permute-start(bf16[2,96,768]{2,1,0:T(8,128)(2,1)} %mask_right.3.refs_0_), channel_id=1, source_target_pairs={{0,2},{1,3},{2,0},{3,1},{4,6},{5,7},{6,4},{7,5},{8,10},{9,11},{10,... | collective-permute-start | bytes 884744 | tf_op jit(solution)/shard_map/ppermute | solution.py:17
  39.7 24.1 %collective-permute-start.26 = (bf16[2,96,768]{2,1,0:T(8,128)(2,1)}, bf16[2,96,768]{2,1,0:T(8,128)(2,1)S(1)}, u32[]{:S(2)}, u32[]{:S(2)}) collective-permute-start(bf16[2,96,768]{2,1,0:T(8,128)(2,1)} %mask_right.3.refs_0_), channel_id=1, source_target_pairs={{0,4},{1,5},{2,6},{3,7},{4,0},{5,1},{6,2},{7,3},{8,12},{9,13},{10,... | collective-permute-start | bytes 884744 | tf_op jit(solution)/shard_map/ppermute | solution.py:17
  43.1 22.2 %collective-permute-start.28 = (bf16[2,96,768]{2,1,0:T(8,128)(2,1)}, bf16[2,96,768]{2,1,0:T(8,128)(2,1)S(1)}, u32[]{:S(2)}, u32[]{:S(2)}) collective-permute-start(bf16[2,96,768]{2,1,0:T(8,128)(2,1)} %mask_right.3.refs_0_), channel_id=1, source_target_pairs={{0,6},{1,7},{2,4},{3,5},{4,2},{5,3},{6,0},{7,1},{8,14},{9,15},{10,... | collective-permute-start | bytes 884744 | tf_op jit(solution)/shard_map/ppermute | solution.py:17
  44.5 22.3 %collective-permute-start.23 = (bf16[2,96,768]{2,1,0:T(8,128)(2,1)}, bf16[2,96,768]{2,1,0:T(8,128)(2,1)S(1)}, u32[]{:S(2)}, u32[]{:S(2)}) collective-permute-start(bf16[2,96,768]{2,1,0:T(8,128)(2,1)} %mask_right.3.refs_0_), channel_id=1, source_target_pairs={{0,1},{1,0},{2,3},{3,2},{4,5},{5,4},{6,7},{7,6},{8,9},{9,8},{10,11... | collective-permute-start | bytes 884744 | tf_op jit(solution)/shard_map/ppermute | solution.py:17
  44.5 22.3 %collective-permute-start.25 = (bf16[2,96,768]{2,1,0:T(8,128)(2,1)S(1)}, bf16[2,96,768]{2,1,0:T(8,128)(2,1)S(1)}, u32[]{:S(2)}, u32[]{:S(2)}) collective-permute-start(bf16[2,96,768]{2,1,0:T(8,128)(2,1)S(1)} %collective-permute-done.24.refs_2_), channel_id=1, source_target_pairs={{0,1},{1,0},{2,3},{3,2},{4,5},{5,4},{6,7},{7,6},{8,9},{9,8},{10,11... | collective-permute-start | bytes 884744 | tf_op jit(solution)/shard_map/ppermute | solution.py:17
  55.2 24.0 %collective-permute-start.17 = (bf16[384,768]{1,0:T(8,128)(2,1)}, bf16[384,768]{1,0:T(8,128)(2,1)S(1)}, u32[]{:S(2)}, u32[]{:S(2)}) collective-permute-start(bf16[384,768]{1,0:T(8,128)(2,1)} %get-tuple-element.37), channel_id=1, source_target_pairs={{0,8},{8,0},{16,24},{24,16},{1,9},{9,1},{17,25},{25,17},{2,10},{10... | collective-permute-start | bytes 1769480 | tf_op jit(solution)/shard_map/ppermute | solution.py:17
  63.8 35.4 %collective-permute-start.18 = (bf16[384,768]{1,0:T(8,128)(2,1)}, bf16[384,768]{1,0:T(8,128)(2,1)S(1)}, u32[]{:S(2)}, u32[]{:S(2)}) collective-permute-start(bf16[384,768]{1,0:T(8,128)(2,1)} %get-tuple-element.38), channel_id=1, source_target_pairs={{0,16},{8,24},{16,0},{24,8},{1,17},{9,25},{17,1},{25,9},{2,18},{10... | collective-permute-start | bytes 1769480 | tf_op jit(solution)/shard_map/ppermute | solution.py:17
  65.3 35.3 %collective-permute-start.19 = (bf16[384,768]{1,0:T(8,128)(2,1)}, bf16[384,768]{1,0:T(8,128)(2,1)S(1)}, u32[]{:S(2)}, u32[]{:S(2)}) collective-permute-start(bf16[384,768]{1,0:T(8,128)(2,1)} %get-tuple-element.39), channel_id=1, source_target_pairs={{0,24},{8,16},{16,8},{24,0},{1,25},{9,17},{17,9},{25,1},{2,26},{10... | collective-permute-start | bytes 1769480 | tf_op jit(solution)/shard_map/ppermute | solution.py:17
  77.1 25.1 %collective-permute-start.30 = (bf16[192,768]{1,0:T(8,128)(2,1)}, bf16[192,768]{1,0:T(8,128)(2,1)S(1)}, u32[]{:S(2)}, u32[]{:S(2)}) collective-permute-start(bf16[192,768]{1,0:T(8,128)(2,1)} %get-tuple-element.42), channel_id=1, source_target_pairs={{0,8},{8,0},{16,24},{24,16},{1,9},{9,1},{17,25},{25,17},{2,10},{10... | collective-permute-start | bytes 884744 | tf_op jit(solution)/shard_map/ppermute | solution.py:17
  77.7 33.3 %collective-permute-start.31 = (bf16[192,768]{1,0:T(8,128)(2,1)}, bf16[192,768]{1,0:T(8,128)(2,1)S(1)}, u32[]{:S(2)}, u32[]{:S(2)}) collective-permute-start(bf16[192,768]{1,0:T(8,128)(2,1)} %get-tuple-element.43), channel_id=1, source_target_pairs={{0,16},{8,24},{16,0},{24,8},{1,17},{9,25},{17,1},{25,9},{2,18},{10... | collective-permute-start | bytes 884744 | tf_op jit(solution)/shard_map/ppermute | solution.py:17
  79.2 31.8 %collective-permute-start.32 = (bf16[192,768]{1,0:T(8,128)(2,1)}, bf16[192,768]{1,0:T(8,128)(2,1)S(1)}, u32[]{:S(2)}, u32[]{:S(2)}) collective-permute-start(bf16[192,768]{1,0:T(8,128)(2,1)} %get-tuple-element.44), channel_id=1, source_target_pairs={{0,24},{8,16},{16,8},{24,0},{1,25},{9,17},{17,9},{25,1},{2,26},{10... | collective-permute-start | bytes 884744 | tf_op jit(solution)/shard_map/ppermute | solution.py:17
  99.2 16.1 %collective-permute-start.52 = (bf16[192,768]{1,0:T(8,128)(2,1)}, bf16[192,768]{1,0:T(8,128)(2,1)S(1)}, u32[]{:S(2)}, u32[]{:S(2)}) collective-permute-start(bf16[192,768]{1,0:T(8,128)(2,1)} %get-tuple-element.53), channel_id=1, source_target_pairs={{0,8},{8,0},{16,24},{24,16},{1,9},{9,1},{17,25},{25,17},{2,10},{10... | collective-permute-start | bytes 884744 | tf_op jit(solution)/shard_map/ppermute | solution.py:17
  100.7 16.1 %collective-permute-start.53 = (bf16[192,768]{1,0:T(8,128)(2,1)}, bf16[192,768]{1,0:T(8,128)(2,1)S(1)}, u32[]{:S(2)}, u32[]{:S(2)}) collective-permute-start(bf16[192,768]{1,0:T(8,128)(2,1)} %get-tuple-element.54), channel_id=1, source_target_pairs={{0,16},{8,24},{16,0},{24,8},{1,17},{9,25},{17,1},{25,9},{2,18},{10... | collective-permute-start | bytes 884744 | tf_op jit(solution)/shard_map/ppermute | solution.py:17
  102.2 14.6 %collective-permute-start.54 = (bf16[192,768]{1,0:T(8,128)(2,1)}, bf16[192,768]{1,0:T(8,128)(2,1)S(1)}, u32[]{:S(2)}, u32[]{:S(2)}) collective-permute-start(bf16[192,768]{1,0:T(8,128)(2,1)} %get-tuple-element.55), channel_id=1, source_target_pairs={{0,24},{8,16},{16,8},{24,0},{1,25},{9,17},{17,9},{25,1},{2,26},{10... | collective-permute-start | bytes 884744 | tf_op jit(solution)/shard_map/ppermute | solution.py:17
  120.8 74.4 %collective-permute-start.55 = (bf16[48,768]{1,0:T(8,128)(2,1)}, bf16[48,768]{1,0:T(8,128)(2,1)S(1)}, u32[]{:S(2)}, u32[]{:S(2)}) collective-permute-start(bf16[48,768]{1,0:T(8,128)(2,1)} %get-tuple-element.56), channel_id=1, source_target_pairs={{0,7},{1,6},{2,5},{3,4},{4,3},{5,2},{6,1},{7,0},{8,15},{9,14},{10,... | collective-permute-start | bytes 221192 | tf_op jit(solution)/shard_map/ppermute | solution.py:17
  130.5 15.7 %collective-permute-start.42 = (bf16[192,768]{1,0:T(8,128)(2,1)S(1)}, bf16[192,768]{1,0:T(8,128)(2,1)S(1)}, u32[]{:S(2)}, u32[]{:S(2)}) collective-permute-start(bf16[192,768]{1,0:T(8,128)(2,1)S(1)} %copy-done.39), channel_id=1, source_target_pairs={{0,16},{8,24},{16,0},{24,8},{1,17},{9,25},{17,1},{25,9},{2,18},{10... | collective-permute-start | bytes 884744 | tf_op jit(solution)/shard_map/ppermute | solution.py:17
  132.7 24.2 %collective-permute-start.47 = (bf16[192,768]{1,0:T(8,128)(2,1)S(1)}, bf16[192,768]{1,0:T(8,128)(2,1)S(1)}, u32[]{:S(2)}, u32[]{:S(2)}) collective-permute-start(bf16[192,768]{1,0:T(8,128)(2,1)S(1)} %copy-done.38), channel_id=1, source_target_pairs={{0,24},{8,16},{16,8},{24,0},{1,25},{9,17},{17,9},{25,1},{2,26},{10... | collective-permute-start | bytes 884744 | tf_op jit(solution)/shard_map/ppermute | solution.py:17
  133.8 61.5 %collective-permute-start.56 = (bf16[48,768]{1,0:T(8,128)(2,1)S(1)}, bf16[48,768]{1,0:T(8,128)(2,1)S(1)}, u32[]{:S(2)}, u32[]{:S(2)}) collective-permute-start(bf16[48,768]{1,0:T(8,128)(2,1)S(1)} %copy-done.47), channel_id=1, source_target_pairs={{0,6},{1,7},{2,4},{3,5},{4,2},{5,3},{6,0},{7,1},{8,14},{9,15},{10,... | collective-permute-start | bytes 221192 | tf_op jit(solution)/shard_map/ppermute | solution.py:17
  135.9 12.1 %collective-permute-start.58 = (bf16[192,768]{1,0:T(8,128)(2,1)S(1)}, bf16[192,768]{1,0:T(8,128)(2,1)S(1)}, u32[]{:S(2)}, u32[]{:S(2)}) collective-permute-start(bf16[192,768]{1,0:T(8,128)(2,1)S(1)} %copy-done.43), channel_id=1, source_target_pairs={{0,8},{8,0},{16,24},{24,16},{1,9},{9,1},{17,25},{25,17},{2,10},{10... | collective-permute-start | bytes 884744 | tf_op jit(solution)/shard_map/ppermute | solution.py:17
  148.0 50.4 %collective-permute-start.57 = (bf16[48,768]{1,0:T(8,128)(2,1)S(1)}, bf16[48,768]{1,0:T(8,128)(2,1)S(1)}, u32[]{:S(2)}, u32[]{:S(2)}) collective-permute-start(bf16[48,768]{1,0:T(8,128)(2,1)S(1)} %copy-done.45), channel_id=1, source_target_pairs={{0,1},{1,0},{2,3},{3,2},{4,5},{5,4},{6,7},{7,6},{8,9},{9,8},{10,11... | collective-permute-start | bytes 221192 | tf_op jit(solution)/shard_map/ppermute | solution.py:17
  (95 other events, 831.9 us)

commit v3 on v2

--- a/solution.py
+++ b/solution.py
@@ -140,8 +140,25 @@
     return [made[k * parts:(k + 1) * parts] for k in range(blocks)]
 
 
+def stack_kernel(*refs):
+    for n, ref in enumerate(refs[:-1]):
+        refs[-1][n] = ref[...]
+
+
+def stacked(sources):
+    full = pl.BlockSpec(memory_space=pltpu.VMEM)
+    return pl.pallas_call(
+        stack_kernel,
+        out_shape=jax.ShapeDtypeStruct((len(sources), *sources[0].shape), jnp.bfloat16),
+        in_specs=[full] * len(sources),
+        out_specs=full,
+        name="stacked",
+    )(*sources)
+
+
 def sum_kernel(targets, *refs, blocks, own_n, steps):
-    sources, outs = refs[:-own_n - blocks], refs[-own_n - blocks:-own_n - 1]
+    sources, outs = refs[1:-own_n - blocks], refs[-own_n - blocks:-own_n - 1]
+    sources = [refs[0].at[n] for n in range(refs[0].shape[0])] + list(sources)
     own, acc = refs[-own_n - 1:-1], refs[-1]
     sub = own[0].shape[0]
     sector = lax.axis_index("sector")
@@ -159,10 +176,11 @@
                 own[step * per + n][...] = acc[0, n * sub:(n + 1) * sub].astype(jnp.bfloat16)
 
 
-def destination_sums(targets, sources, starts, blocks, rows, own_n, steps):
+def destination_sums(targets, early, sources, start, blocks, rows, own_n, steps):
     width = sources[0].shape[1]
     step, sub = rows // steps, rows // own_n
-    specs = [pl.BlockSpec((step, width), lambda n, at=at // step: (n + at, 0)) for at in starts]
+    specs = [pl.BlockSpec((early.shape[0], step, width), lambda n: (0, n + start // step, 0))]
+    specs += [pl.BlockSpec((step, width), lambda n: (n, 0))] * len(sources)
     return pl.pallas_call(
         functools.partial(sum_kernel, blocks=blocks, own_n=own_n, steps=steps),
         grid=(steps,),
@@ -173,7 +191,7 @@
         + [pl.BlockSpec((sub, width), lambda n: (0, 0))] * own_n,
         scratch_shapes=[pltpu.VMEM((blocks, step, width), jnp.float32)],
         name="destination_sums",
-    )(targets, *sources)
+    )(targets, early, *sources)
 
 
 def fast(*arrays):
@@ -208,12 +226,11 @@
             for k in range(blocks)])
 
     placed = []
+    early = stacked([part for channel in received[:-1] for parts in channel for part in parts])
     for u, chunk in enumerate(shard_chunks(shards_n)):
         chunk_rows = len(chunk) * sub
-        parts = [parts for channel in received for parts in channel]
         totals = destination_sums(
-            targets, [p[u % len(p)] for p in parts], [0 if len(p) > 1 else u * chunk_rows for p in parts],
-            blocks, chunk_rows, len(chunk), 1 + len(chunk) % 2 * (len(chunk) - 1) if len(chunk) % 2 else 2)
+            targets, early, [parts[u] for parts in received[-1]], u * chunk_rows, blocks, chunk_rows, len(chunk), 2)
         for j in range(blocks):
             row_at = (own_row ^ (j // col_parts)) * sub
             col_at = (own_col ^ (j % col_parts)) * bond

time: 213 us -> 214 us (level)
  waiting for transfers between devices: 113 us -> 107 us
  starting transfers between devices: 63 us -> 67.2 us
  Pallas kernels: 27.2 us -> 30 us
    ppermute x70, waiting for transfers between devices: 113 us -> 107 us  [exchange(): return lax.ppermute(x, axis, [(a, a ^ offset) for a in range(size)])]
    ppermute x70, starting transfers between devices: 63 us -> 67.2 us  [exchange(): return lax.ppermute(x, axis, [(a, a ^ offset) for a in range(size)])]
    pallas_call x0 -> x1, Pallas kernels: none -> 3.16 us  [stacked(): pl.pallas_call(stack_kernel, out_shape=jax.ShapeDtypeStruct((len(sources)...]
  transfers between devices with their start and end apart: 70 -> 70, of which waited for: 30 -> 27; matrix products, arithmetic and copies ran while one was open for 0% -> 0% of each run, Pallas kernels for 12% -> 13%
where the time goes in v3:
time: 214 us; the launch traced here: 212 us
  waiting for transfers between devices  107 us (50%)
  starting transfers between devices  67.2 us (31%)
  Pallas kernels  30 us (14%)
  local copies, waits for them, and re-layouts  6.66 us (3%)
    ppermute x70, waiting for transfers between devices, exchange(): return lax.ppermute(x, axis, [(a, a ^ offset) for a in range(size)])  107 us
    ppermute x70, starting transfers between devices, exchange(): return lax.ppermute(x, axis, [(a, a ^ offset) for a in range(size)])  67.2 us
    pallas_call x2, Pallas kernels, products(): pl.pallas_call(functools.partial(products_kernel, shards_n=shards_n, row_...  14.9 us
    pallas_call x2, Pallas kernels, destination_sums(): pl.pallas_call(functools.partial(sum_kernel, blocks=blocks, own_n=own_n,...  6.02 us
    unnamed x98, local copies, waits for them, and re-layouts  5.41 us
  transfers between devices with their start and end apart: 70, of which 27 were waited for; matrix products, arithmetic and copies ran while one was open for 0% of the time, Pallas kernels for 13%

profile of v3, /device:TPU:0, one launch (start us, length us, event | category | flops | bytes accessed | tf_op | source)
XLA Modules:
  0.0 212.1 jit_solution(10148048121932193278)
XLA Ops:
  1.8 3.0 %collective-permute-start.7 = (bf16[96,768]{1,0:T(8,128)(2,1)}, bf16[96,768]{1,0:T(8,128)(2,1)S(1)}, u32[]{:S(2)}, u32[]{:S(2)}) collective-permute-start(bf16[96,768]{1,0:T(8,128)(2,1)} %get-tuple-element.35.refs_0_), channel_id=1, source_target_pairs={{0,8},{8,0},{16,24},{24,16},{1,9},{9,1},{17,25},{25,17},{2,10},{10... | collective-permute-start | bytes 442376 | tf_op jit(solution)/shard_map/ppermute | solution.py:17
  17.0 4.9 %collective-permute-done.3.refs_4_ = bf16[96,768]{1,0:T(8,128)(2,1)S(1)} collective-permute-done((bf16[96,768]{1,0:T(8,128)(2,1)}, bf16[96,768]{1,0:T(8,128)(2,1)S(1)}, u32[]{:S(2)}, u32[]{:S(2)}) %collective-permute-start.3) | collective-permute-done | bytes 147488 | tf_op jit(solution)/shard_map/ppermute | solution.py:17
  33.1 5.2 %collective-permute-done.13.refs_12_ = bf16[96,768]{1,0:T(8,128)(2,1)S(1)} collective-permute-done((bf16[96,768]{1,0:T(8,128)(2,1)}, bf16[96,768]{1,0:T(8,128)(2,1)S(1)}, u32[]{:S(2)}, u32[]{:S(2)}) %collective-permute-start.13) | collective-permute-done | bytes 147488 | tf_op jit(solution)/shard_map/ppermute | solution.py:17
  39.7 3.4 %collective-permute-start.26 = (bf16[2,96,768]{2,1,0:T(8,128)(2,1)}, bf16[2,96,768]{2,1,0:T(8,128)(2,1)S(1)}, u32[]{:S(2)}, u32[]{:S(2)}) collective-permute-start(bf16[2,96,768]{2,1,0:T(8,128)(2,1)} %mask_right.3.refs_0_), channel_id=1, source_target_pairs={{0,4},{1,5},{2,6},{3,7},{4,0},{5,1},{6,2},{7,3},{8,12},{9,13},{10,... | collective-permute-start | bytes 884744 | tf_op jit(solution)/shard_map/ppermute | solution.py:17
  47.6 7.6 %products.2 = (bf16[384,768]{1,0:T(8,128)(2,1)}, bf16[384,768]{1,0:T(8,128)(2,1)}, bf16[384,768]{1,0:T(8,128)(2,1)}, bf16[384,768]{1,0:T(8,128)(2,1)}) custom-call(bf16[96,768]{1,0:T(8,128)(2,1)} %get-tuple-element.34.refs_0_, bf16[96,768]{1,0:T(8,128)(2,1)} %copy-done.20, bf16[96,768]{1,0:T(8,128)(2,1)} %copy-done.17, bf16[96,768]{1,0:T(8,128)(2,1)} %copy-done.25, ...), custom_call_target="tpu_custom_call" | custom-call | tf_op jit(solution)/shard_map/products/pallas_call | solution.py:131
  56.8 7.1 %collective-permute-done.26.refs_4_ = bf16[2,96,768]{2,1,0:T(8,128)(2,1)S(1)} collective-permute-done((bf16[2,96,768]{2,1,0:T(8,128)(2,1)}, bf16[2,96,768]{2,1,0:T(8,128)(2,1)S(1)}, u32[]{:S(2)}, u32[]{:S(2)}) %collective-permute-start.26) | collective-permute-done | bytes 294944 | tf_op jit(solution)/shard_map/ppermute | solution.py:17
  69.8 7.3 %products.3 = (bf16[192,768]{1,0:T(8,128)(2,1)}, bf16[192,768]{1,0:T(8,128)(2,1)}, bf16[192,768]{1,0:T(8,128)(2,1)}, bf16[192,768]{1,0:T(8,128)(2,1)}, bf16[192,...) custom-call(bf16[2,96,768]{2,1,0:T(8,128)(2,1)} %mask_right.3.refs_0_, ...), custom_call_target="tpu_custom_call" | custom-call | tf_op jit(solution)/shard_map/products/pallas_call | solution.py:131
  80.6 18.6 %collective-permute-done.18.refs_2_ = bf16[384,768]{1,0:T(8,128)(2,1)S(1)} collective-permute-done((bf16[384,768]{1,0:T(8,128)(2,1)}, bf16[384,768]{1,0:T(8,128)(2,1)S(1)}, u32[]{:S(2)}, u32[]{:S(2)}) %collective-permute-start.18) | collective-permute-done | bytes 589856 | tf_op jit(solution)/shard_map/ppermute | solution.py:17
  102.7 3.2 %stacked.1.refs_0_ = bf16[4,384,768]{2,1,0:T(8,128)(2,1)} custom-call(bf16[384,768]{1,0:T(8,128)(2,1)} %get-tuple-element.36.refs_0_, bf16[384,768]{1,0:T(8,128)(2,1)} %copy-done.1, bf16[384,768]{1,0:T(8,128)(2,1)} %copy-done.2, bf16[384,768]{1,0:T(8,128)(2,1)} %copy-done.3), custom_call_target="tpu_custom_call" | custom-call | tf_op jit(solution)/shard_map/stacked/pallas_call | solution.py:150
  105.9 5.1 %collective-permute-done.31.refs_3_ = bf16[192,768]{1,0:T(8,128)(2,1)S(1)} collective-permute-done((bf16[192,768]{1,0:T(8,128)(2,1)}, bf16[192,768]{1,0:T(8,128)(2,1)S(1)}, u32[]{:S(2)}, u32[]{:S(2)}) %collective-permute-start.31) | collective-permute-done | bytes 294944 | tf_op jit(solution)/shard_map/ppermute | solution.py:17
  111.8 3.0 %destination_sums.2 = (bf16[192,768]{1,0:T(8,128)(2,1)}, bf16[192,768]{1,0:T(8,128)(2,1)}, bf16[192,768]{1,0:T(8,128)(2,1)}, bf16[48,768]{1,0:T(8,128)(2,1)}, bf...) custom-call(s32[2,4]{1,0:T(2,128)} %targets.9, bf16[4,384,768]{2,1,0:T(8,128)(2,1)} %stacked.1.refs_0_, ...), custom_call_target="tpu_custom_call" | custom-call | tf_op jit(solution)/shard_map/destination_sums/pallas_call | solution.py:184
  117.6 3.0 %destination_sums.3 = (bf16[192,768]{1,0:T(8,128)(2,1)}, bf16[192,768]{1,0:T(8,128)(2,1)}, bf16[192,768]{1,0:T(8,128)(2,1)}, bf16[48,768]{1,0:T(8,128)(2,1)}, bf...) custom-call(s32[2,4]{1,0:T(2,128)} %targets.9, bf16[4,384,768]{2,1,0:T(8,128)(2,1)} %stacked.1.refs_0_, ...), custom_call_target="tpu_custom_call" | custom-call | tf_op jit(solution)/shard_map/destination_sums/pallas_call | solution.py:184
  126.6 3.6 %collective-permute-done.34 = bf16[48,768]{1,0:T(8,128)(2,1)S(1)} collective-permute-done((bf16[48,768]{1,0:T(8,128)(2,1)S(1)}, bf16[48,768]{1,0:T(8,128)(2,1)S(1)}, u32[]{:S(2)}, u32[]{:S(2)}) %collective-permute-start.34) | collective-permute-done | bytes 73760 | tf_op jit(solution)/shard_map/ppermute | solution.py:17
  136.3 9.5 %collective-permute-done.42 = bf16[192,768]{1,0:T(8,128)(2,1)S(1)} collective-permute-done((bf16[192,768]{1,0:T(8,128)(2,1)S(1)}, bf16[192,768]{1,0:T(8,128)(2,1)S(1)}, u32[]{:S(2)}, u32[]{:S(2)}) %collective-permute-start.42) | collective-permute-done | bytes 294944 | tf_op jit(solution)/shard_map/ppermute | solution.py:17
  147.7 6.3 %collective-permute-done.62 = bf16[192,768]{1,0:T(8,128)(2,1)S(1)} collective-permute-done((bf16[192,768]{1,0:T(8,128)(2,1)S(1)}, bf16[192,768]{1,0:T(8,128)(2,1)S(1)}, u32[]{:S(2)}, u32[]{:S(2)}) %collective-permute-start.62) | collective-permute-done | bytes 294944 | tf_op jit(solution)/shard_map/ppermute | solution.py:17
  156.7 5.6 %collective-permute-done.66 = bf16[192,768]{1,0:T(8,128)(2,1)S(1)} collective-permute-done((bf16[192,768]{1,0:T(8,128)(2,1)S(1)}, bf16[192,768]{1,0:T(8,128)(2,1)S(1)}, u32[]{:S(2)}, u32[]{:S(2)}) %collective-permute-start.66) | collective-permute-done | bytes 294944 | tf_op jit(solution)/shard_map/ppermute | solution.py:17
  162.6 5.2 %collective-permute-done.39 = bf16[48,768]{1,0:T(8,128)(2,1)S(1)} collective-permute-done((bf16[48,768]{1,0:T(8,128)(2,1)S(1)}, bf16[48,768]{1,0:T(8,128)(2,1)S(1)}, u32[]{:S(2)}, u32[]{:S(2)}) %collective-permute-start.39) | collective-permute-done | bytes 73760 | tf_op jit(solution)/shard_map/ppermute | solution.py:17
  168.5 3.0 %collective-permute-done.41 = bf16[48,768]{1,0:T(8,128)(2,1)S(1)} collective-permute-done((bf16[48,768]{1,0:T(8,128)(2,1)S(1)}, bf16[48,768]{1,0:T(8,128)(2,1)S(1)}, u32[]{:S(2)}, u32[]{:S(2)}) %collective-permute-start.41) | collective-permute-done | bytes 73760 | tf_op jit(solution)/shard_map/ppermute | solution.py:17
  172.5 4.6 %collective-permute-done.43 = bf16[48,768]{1,0:T(8,128)(2,1)S(1)} collective-permute-done((bf16[48,768]{1,0:T(8,128)(2,1)S(1)}, bf16[48,768]{1,0:T(8,128)(2,1)S(1)}, u32[]{:S(2)}, u32[]{:S(2)}) %collective-permute-start.43) | collective-permute-done | bytes 73760 | tf_op jit(solution)/shard_map/ppermute | solution.py:17
  177.8 4.2 %collective-permute-done.45 = bf16[48,768]{1,0:T(8,128)(2,1)S(1)} collective-permute-done((bf16[48,768]{1,0:T(8,128)(2,1)S(1)}, bf16[48,768]{1,0:T(8,128)(2,1)S(1)}, u32[]{:S(2)}, u32[]{:S(2)}) %collective-permute-start.45) | collective-permute-done | bytes 73760 | tf_op jit(solution)/shard_map/ppermute | solution.py:17
  182.4 7.1 %collective-permute-done.48 = bf16[48,768]{1,0:T(8,128)(2,1)S(1)} collective-permute-done((bf16[48,768]{1,0:T(8,128)(2,1)S(1)}, bf16[48,768]{1,0:T(8,128)(2,1)S(1)}, u32[]{:S(2)}, u32[]{:S(2)}) %collective-permute-start.48) | collective-permute-done | bytes 73760 | tf_op jit(solution)/shard_map/ppermute | solution.py:17
  189.6 4.5 %collective-permute-done.50 = bf16[48,768]{1,0:T(8,128)(2,1)S(1)} collective-permute-done((bf16[48,768]{1,0:T(8,128)(2,1)S(1)}, bf16[48,768]{1,0:T(8,128)(2,1)S(1)}, u32[]{:S(2)}, u32[]{:S(2)}) %collective-permute-start.50) | collective-permute-done | bytes 73760 | tf_op jit(solution)/shard_map/ppermute | solution.py:17
  198.3 3.2 %collective-permute-start.64 = (bf16[48,768]{1,0:T(8,128)(2,1)S(1)}, bf16[48,768]{1,0:T(8,128)(2,1)S(1)}, u32[]{:S(2)}, u32[]{:S(2)}) collective-permute-start(bf16[48,768]{1,0:T(8,128)(2,1)S(1)} %get-tuple-element.67), channel_id=1, source_target_pairs={{0,6},{1,7},{2,4},{3,5},{4,2},{5,3},{6,0},{7,1},{8,14},{9,15},{10,... | collective-permute-start | bytes 221192 | tf_op jit(solution)/shard_map/ppermute | solution.py:17
  202.9 2.9 %collective-permute-start.68 = (bf16[48,768]{1,0:T(8,128)(2,1)S(1)}, bf16[48,768]{1,0:T(8,128)(2,1)S(1)}, u32[]{:S(2)}, u32[]{:S(2)}) collective-permute-start(bf16[48,768]{1,0:T(8,128)(2,1)S(1)} %get-tuple-element.64), channel_id=1, source_target_pairs={{0,6},{1,7},{2,4},{3,5},{4,2},{5,3},{6,0},{7,1},{8,14},{9,15},{10,... | collective-permute-start | bytes 221192 | tf_op jit(solution)/shard_map/ppermute | solution.py:17
  (261 shorter events, 80.2 us)
Async XLA Ops:
  8.4 13.5 %collective-permute-start.3 = (bf16[96,768]{1,0:T(8,128)(2,1)}, bf16[96,768]{1,0:T(8,128)(2,1)S(1)}, u32[]{:S(2)}, u32[]{:S(2)}) collective-permute-start(bf16[96,768]{1,0:T(8,128)(2,1)} %get-tuple-element.34.refs_0_), channel_id=1, source_target_pairs={{0,4},{1,5},{2,6},{3,7},{4,0},{5,1},{6,2},{7,3},{8,12},{9,13},{10,... | collective-permute-start | bytes 442376 | tf_op jit(solution)/shard_map/ppermute | solution.py:17
  11.0 12.9 %collective-permute-start.5 = (bf16[96,768]{1,0:T(8,128)(2,1)}, bf16[96,768]{1,0:T(8,128)(2,1)S(1)}, u32[]{:S(2)}, u32[]{:S(2)}) collective-permute-start(bf16[96,768]{1,0:T(8,128)(2,1)} %get-tuple-element.34.refs_0_), channel_id=1, source_target_pairs={{0,6},{1,7},{2,4},{3,5},{4,2},{5,3},{6,0},{7,1},{8,14},{9,15},{10,... | collective-permute-start | bytes 442376 | tf_op jit(solution)/shard_map/ppermute | solution.py:17
  15.3 11.6 %collective-permute-start.21 = (bf16[96,768]{1,0:T(8,128)(2,1)}, bf16[96,768]{1,0:T(8,128)(2,1)S(1)}, u32[]{:S(2)}, u32[]{:S(2)}) collective-permute-start(bf16[96,768]{1,0:T(8,128)(2,1)} %get-tuple-element.40.refs_0_), channel_id=1, source_target_pairs={{0,16},{8,24},{16,0},{24,8},{1,17},{9,25},{17,1},{25,9},{2,18},{10... | collective-permute-start | bytes 442376 | tf_op jit(solution)/shard_map/ppermute | solution.py:17
  24.1 14.3 %collective-permute-start.13 = (bf16[96,768]{1,0:T(8,128)(2,1)}, bf16[96,768]{1,0:T(8,128)(2,1)S(1)}, u32[]{:S(2)}, u32[]{:S(2)}) collective-permute-start(bf16[96,768]{1,0:T(8,128)(2,1)} %mask_right.2.refs_8_), channel_id=1, source_target_pairs={{0,4},{1,5},{2,6},{3,7},{4,0},{5,1},{6,2},{7,3},{8,12},{9,13},{10,... | collective-permute-start | bytes 442376 | tf_op jit(solution)/shard_map/ppermute | solution.py:17
  31.2 13.3 %collective-permute-start.24 = (bf16[2,96,768]{2,1,0:T(8,128)(2,1)}, bf16[2,96,768]{2,1,0:T(8,128)(2,1)S(1)}, u32[]{:S(2)}, u32[]{:S(2)}) collective-permute-start(bf16[2,96,768]{2,1,0:T(8,128)(2,1)} %mask_right.3.refs_0_), channel_id=1, source_target_pairs={{0,2},{1,3},{2,0},{3,1},{4,6},{5,7},{6,4},{7,5},{8,10},{9,11},{10,... | collective-permute-start | bytes 884744 | tf_op jit(solution)/shard_map/ppermute | solution.py:17
  39.7 24.1 %collective-permute-start.26 = (bf16[2,96,768]{2,1,0:T(8,128)(2,1)}, bf16[2,96,768]{2,1,0:T(8,128)(2,1)S(1)}, u32[]{:S(2)}, u32[]{:S(2)}) collective-permute-start(bf16[2,96,768]{2,1,0:T(8,128)(2,1)} %mask_right.3.refs_0_), channel_id=1, source_target_pairs={{0,4},{1,5},{2,6},{3,7},{4,0},{5,1},{6,2},{7,3},{8,12},{9,13},{10,... | collective-permute-start | bytes 884744 | tf_op jit(solution)/shard_map/ppermute | solution.py:17
  43.1 22.2 %collective-permute-start.28 = (bf16[2,96,768]{2,1,0:T(8,128)(2,1)}, bf16[2,96,768]{2,1,0:T(8,128)(2,1)S(1)}, u32[]{:S(2)}, u32[]{:S(2)}) collective-permute-start(bf16[2,96,768]{2,1,0:T(8,128)(2,1)} %mask_right.3.refs_0_), channel_id=1, source_target_pairs={{0,6},{1,7},{2,4},{3,5},{4,2},{5,3},{6,0},{7,1},{8,14},{9,15},{10,... | collective-permute-start | bytes 884744 | tf_op jit(solution)/shard_map/ppermute | solution.py:17
  44.5 22.3 %collective-permute-start.23 = (bf16[2,96,768]{2,1,0:T(8,128)(2,1)}, bf16[2,96,768]{2,1,0:T(8,128)(2,1)S(1)}, u32[]{:S(2)}, u32[]{:S(2)}) collective-permute-start(bf16[2,96,768]{2,1,0:T(8,128)(2,1)} %mask_right.3.refs_0_), channel_id=1, source_target_pairs={{0,1},{1,0},{2,3},{3,2},{4,5},{5,4},{6,7},{7,6},{8,9},{9,8},{10,11... | collective-permute-start | bytes 884744 | tf_op jit(solution)/shard_map/ppermute | solution.py:17
  44.5 22.3 %collective-permute-start.25 = (bf16[2,96,768]{2,1,0:T(8,128)(2,1)S(1)}, bf16[2,96,768]{2,1,0:T(8,128)(2,1)S(1)}, u32[]{:S(2)}, u32[]{:S(2)}) collective-permute-start(bf16[2,96,768]{2,1,0:T(8,128)(2,1)S(1)} %collective-permute-done.24.refs_2_), channel_id=1, source_target_pairs={{0,1},{1,0},{2,3},{3,2},{4,5},{5,4},{6,7},{7,6},{8,9},{9,8},{10,11... | collective-permute-start | bytes 884744 | tf_op jit(solution)/shard_map/ppermute | solution.py:17
  55.2 24.0 %collective-permute-start.17 = (bf16[384,768]{1,0:T(8,128)(2,1)}, bf16[384,768]{1,0:T(8,128)(2,1)S(1)}, u32[]{:S(2)}, u32[]{:S(2)}) collective-permute-start(bf16[384,768]{1,0:T(8,128)(2,1)} %get-tuple-element.37), channel_id=1, source_target_pairs={{0,8},{8,0},{16,24},{24,16},{1,9},{9,1},{17,25},{25,17},{2,10},{10... | collective-permute-start | bytes 1769480 | tf_op jit(solution)/shard_map/ppermute | solution.py:17
  63.8 35.4 %collective-permute-start.18 = (bf16[384,768]{1,0:T(8,128)(2,1)}, bf16[384,768]{1,0:T(8,128)(2,1)S(1)}, u32[]{:S(2)}, u32[]{:S(2)}) collective-permute-start(bf16[384,768]{1,0:T(8,128)(2,1)} %get-tuple-element.38), channel_id=1, source_target_pairs={{0,16},{8,24},{16,0},{24,8},{1,17},{9,25},{17,1},{25,9},{2,18},{10... | collective-permute-start | bytes 1769480 | tf_op jit(solution)/shard_map/ppermute | solution.py:17
  65.4 35.3 %collective-permute-start.19 = (bf16[384,768]{1,0:T(8,128)(2,1)}, bf16[384,768]{1,0:T(8,128)(2,1)S(1)}, u32[]{:S(2)}, u32[]{:S(2)}) collective-permute-start(bf16[384,768]{1,0:T(8,128)(2,1)} %get-tuple-element.39), channel_id=1, source_target_pairs={{0,24},{8,16},{16,8},{24,0},{1,25},{9,17},{17,9},{25,1},{2,26},{10... | collective-permute-start | bytes 1769480 | tf_op jit(solution)/shard_map/ppermute | solution.py:17
  77.1 25.1 %collective-permute-start.30 = (bf16[192,768]{1,0:T(8,128)(2,1)}, bf16[192,768]{1,0:T(8,128)(2,1)S(1)}, u32[]{:S(2)}, u32[]{:S(2)}) collective-permute-start(bf16[192,768]{1,0:T(8,128)(2,1)} %get-tuple-element.42), channel_id=1, source_target_pairs={{0,8},{8,0},{16,24},{24,16},{1,9},{9,1},{17,25},{25,17},{2,10},{10... | collective-permute-start | bytes 884744 | tf_op jit(solution)/shard_map/ppermute | solution.py:17
  77.7 33.3 %collective-permute-start.31 = (bf16[192,768]{1,0:T(8,128)(2,1)}, bf16[192,768]{1,0:T(8,128)(2,1)S(1)}, u32[]{:S(2)}, u32[]{:S(2)}) collective-permute-start(bf16[192,768]{1,0:T(8,128)(2,1)} %get-tuple-element.43), channel_id=1, source_target_pairs={{0,16},{8,24},{16,0},{24,8},{1,17},{9,25},{17,1},{25,9},{2,18},{10... | collective-permute-start | bytes 884744 | tf_op jit(solution)/shard_map/ppermute | solution.py:17
  79.2 31.8 %collective-permute-start.32 = (bf16[192,768]{1,0:T(8,128)(2,1)}, bf16[192,768]{1,0:T(8,128)(2,1)S(1)}, u32[]{:S(2)}, u32[]{:S(2)}) collective-permute-start(bf16[192,768]{1,0:T(8,128)(2,1)} %get-tuple-element.44), channel_id=1, source_target_pairs={{0,24},{8,16},{16,8},{24,0},{1,25},{9,17},{17,9},{25,1},{2,26},{10... | collective-permute-start | bytes 884744 | tf_op jit(solution)/shard_map/ppermute | solution.py:17
  99.2 15.9 %collective-permute-start.52 = (bf16[192,768]{1,0:T(8,128)(2,1)}, bf16[192,768]{1,0:T(8,128)(2,1)S(1)}, u32[]{:S(2)}, u32[]{:S(2)}) collective-permute-start(bf16[192,768]{1,0:T(8,128)(2,1)} %get-tuple-element.53), channel_id=1, source_target_pairs={{0,8},{8,0},{16,24},{24,16},{1,9},{9,1},{17,25},{25,17},{2,10},{10... | collective-permute-start | bytes 884744 | tf_op jit(solution)/shard_map/ppermute | solution.py:17
  100.7 16.1 %collective-permute-start.53 = (bf16[192,768]{1,0:T(8,128)(2,1)}, bf16[192,768]{1,0:T(8,128)(2,1)S(1)}, u32[]{:S(2)}, u32[]{:S(2)}) collective-permute-start(bf16[192,768]{1,0:T(8,128)(2,1)} %get-tuple-element.54), channel_id=1, source_target_pairs={{0,16},{8,24},{16,0},{24,8},{1,17},{9,25},{17,1},{25,9},{2,18},{10... | collective-permute-start | bytes 884744 | tf_op jit(solution)/shard_map/ppermute | solution.py:17
  102.2 14.6 %collective-permute-start.54 = (bf16[192,768]{1,0:T(8,128)(2,1)}, bf16[192,768]{1,0:T(8,128)(2,1)S(1)}, u32[]{:S(2)}, u32[]{:S(2)}) collective-permute-start(bf16[192,768]{1,0:T(8,128)(2,1)} %get-tuple-element.55), channel_id=1, source_target_pairs={{0,24},{8,16},{16,8},{24,0},{1,25},{9,17},{17,9},{25,1},{2,26},{10... | collective-permute-start | bytes 884744 | tf_op jit(solution)/shard_map/ppermute | solution.py:17
  120.7 74.9 %collective-permute-start.55 = (bf16[48,768]{1,0:T(8,128)(2,1)}, bf16[48,768]{1,0:T(8,128)(2,1)S(1)}, u32[]{:S(2)}, u32[]{:S(2)}) collective-permute-start(bf16[48,768]{1,0:T(8,128)(2,1)} %get-tuple-element.56), channel_id=1, source_target_pairs={{0,7},{1,6},{2,5},{3,4},{4,3},{5,2},{6,1},{7,0},{8,15},{9,14},{10,... | collective-permute-start | bytes 221192 | tf_op jit(solution)/shard_map/ppermute | solution.py:17
  130.3 15.6 %collective-permute-start.42 = (bf16[192,768]{1,0:T(8,128)(2,1)S(1)}, bf16[192,768]{1,0:T(8,128)(2,1)S(1)}, u32[]{:S(2)}, u32[]{:S(2)}) collective-permute-start(bf16[192,768]{1,0:T(8,128)(2,1)S(1)} %copy-done.39), channel_id=1, source_target_pairs={{0,16},{8,24},{16,0},{24,8},{1,17},{9,25},{17,1},{25,9},{2,18},{10... | collective-permute-start | bytes 884744 | tf_op jit(solution)/shard_map/ppermute | solution.py:17
  132.5 24.0 %collective-permute-start.47 = (bf16[192,768]{1,0:T(8,128)(2,1)S(1)}, bf16[192,768]{1,0:T(8,128)(2,1)S(1)}, u32[]{:S(2)}, u32[]{:S(2)}) collective-permute-start(bf16[192,768]{1,0:T(8,128)(2,1)S(1)} %copy-done.38), channel_id=1, source_target_pairs={{0,24},{8,16},{16,8},{24,0},{1,25},{9,17},{17,9},{25,1},{2,26},{10... | collective-permute-start | bytes 884744 | tf_op jit(solution)/shard_map/ppermute | solution.py:17
  133.5 64.4 %collective-permute-start.56 = (bf16[48,768]{1,0:T(8,128)(2,1)S(1)}, bf16[48,768]{1,0:T(8,128)(2,1)S(1)}, u32[]{:S(2)}, u32[]{:S(2)}) collective-permute-start(bf16[48,768]{1,0:T(8,128)(2,1)S(1)} %copy-done.47), channel_id=1, source_target_pairs={{0,6},{1,7},{2,4},{3,5},{4,2},{5,3},{6,0},{7,1},{8,14},{9,15},{10,... | collective-permute-start | bytes 221192 | tf_op jit(solution)/shard_map/ppermute | solution.py:17
  135.4 12.2 %collective-permute-start.58 = (bf16[192,768]{1,0:T(8,128)(2,1)S(1)}, bf16[192,768]{1,0:T(8,128)(2,1)S(1)}, u32[]{:S(2)}, u32[]{:S(2)}) collective-permute-start(bf16[192,768]{1,0:T(8,128)(2,1)S(1)} %copy-done.43), channel_id=1, source_target_pairs={{0,8},{8,0},{16,24},{24,16},{1,9},{9,1},{17,25},{25,17},{2,10},{10... | collective-permute-start | bytes 884744 | tf_op jit(solution)/shard_map/ppermute | solution.py:17
  147.6 50.7 %collective-permute-start.57 = (bf16[48,768]{1,0:T(8,128)(2,1)S(1)}, bf16[48,768]{1,0:T(8,128)(2,1)S(1)}, u32[]{:S(2)}, u32[]{:S(2)}) collective-permute-start(bf16[48,768]{1,0:T(8,128)(2,1)S(1)} %copy-done.45), channel_id=1, source_target_pairs={{0,1},{1,0},{2,3},{3,2},{4,5},{5,4},{6,7},{7,6},{8,9},{9,8},{10,11... | collective-permute-start | bytes 221192 | tf_op jit(solution)/shard_map/ppermute | solution.py:17
  (95 other events, 807.2 us)
